TPU v7x, 512 devices: a whole 4x8x8 slice. The times are simulated.
512 devices in a mesh: ctx: 16 (over y, core), db: 4 (over z_lo), tp: 8 (over x, z_hi).
Axes of the slice: x: 4, y: 8, z: 8 (z_hi: 2, z_lo: 4; z = z_hi * 4 + z_lo), core: 2. Of those that a mesh axis runs over, the one named last changes fastest.
Arguments:
- hidden_in: bfloat16 [4, 4096, 4096], P('db', 'ctx', 'tp'), may hold values from -6 to 6
- queries: bfloat16 [4, 4096, 4096], P('db', 'ctx', 'tp')
- keys: bfloat16 [4, 4096, 4096], P('db', 'ctx', 'tp')
- values: bfloat16 [4, 4096, 4096], P('db', 'ctx', 'tp'), may hold values from -6 to 6
- cross_queries: bfloat16 [4, 4096, 4096], P('db', 'ctx', 'tp')
- neighbours: int32 [4, 64, 2], P('db', 'ctx'), may hold values from 0 to 31, as said below
- database: bfloat16 [2, 32, 128, 4096], P(None, 'db', None, 'tp')
- out_weight: bfloat16 [4096, 4096], P('tp', 'db'), may hold values from -0.125 to 0.125
Outputs:
- attended: bfloat16 [4, 4096, 4096], P('db', 'ctx', 'tp')
- mixed: bfloat16 [4, 4096, 4096], P('db', 'ctx', 'tp')
Inputs may be any that keep to these rules, and one draw needn't show every extreme that they name: `neighbours`: block id n is held by database shard n // 8. Among the 8 entries of the retrieval blocks of each aligned run of 256 positions of a sequence, no shard holds more than 4, and one shard holds exactly 4; in each such run of positions this shard is the same for all sequences.
All inputs are finite; a program needn't handle non-finite values.
Results may differ from a plain program's by a relative error of at most 0.007.
Values may be sent and summed in bfloat16 or wider, within the bound.
A program may use at most 64 MiB of HBM per device.

v0:
```python
import math

import jax
import jax.numpy as jnp
from jax import lax
from jax.sharding import PartitionSpec as P

DH = 128
SPAN = 64


def passed_along(value, axis, steps):
    count = lax.axis_size(axis)
    leading, last = (max(0, -steps), min(count, count - steps))
    return lax.ppermute(value, axis, [(source, source + steps) for source in range(leading, last)])


def shards(hidden_in, queries, keys, values, cross_queries, neighbours, database, out_weight):
    rows_here = queries.shape[1]
    width_here = queries.shape[2]
    head_count = width_here // DH
    scale = 1.0 / math.sqrt(DH)
    member_count = lax.axis_size("ctx")
    member = lax.axis_index("ctx")
    row_index = jnp.arange(rows_here, dtype=jnp.int32)
    query_pos = member * rows_here + row_index

    def split_heads(array):
        return array[0].reshape(rows_here, head_count, DH).transpose(1, 0, 2)

    query_heads = split_heads(queries)
    moving_all = jnp.stack([split_heads(keys), split_heads(values)])

    def absorb(state, query_part, moving, source):
        best_so, total_so, accum_so = state
        key_pos = source * rows_here + row_index
        score = (
            jnp.einsum("hqd,hkd->hqk", query_part, moving[0], preferred_element_type=jnp.float32)
            * scale
        )
        allowed = (key_pos[None, :] <= query_pos[:, None])[None]
        peak = jnp.maximum(best_so, jnp.max(jnp.where(allowed, score, -1e30), axis=-1))
        weights = jnp.where(allowed, jnp.exp(score - peak[..., None]), 0.0)
        factor = jnp.exp(best_so - peak)
        total_new = total_so * factor + jnp.sum(weights, axis=-1)
        accum_new = accum_so * factor[..., None] + jnp.einsum(
            "hqk,hkd->hqd",
            weights.astype(jnp.bfloat16),
            moving[1],
            preferred_element_type=jnp.float32,
        )
        return (peak, total_new, accum_new)

    def advance(turn_index, carry):
        moving, state = carry
        state = absorb(state, query_heads, moving, (member - turn_index) % member_count)
        moving = passed_along(moving, "ctx", 1)
        return (moving, state)

    moving, state = lax.fori_loop(
        0,
        member_count - 1,
        advance,
        (
            moving_all,
            (
                jnp.full((head_count, rows_here), -1e30, jnp.float32),
                jnp.zeros((head_count, rows_here), jnp.float32),
                jnp.zeros((head_count, rows_here, DH), jnp.float32),
            ),
        ),
    )
    state = absorb(state, query_heads, moving, (member - member_count + 1) % member_count)
    total_final = state[1]
    accum_final = state[2]
    attended = (
        (accum_final / total_final[..., None])
        .astype(jnp.bfloat16)
        .transpose(1, 0, 2)
        .reshape(1, rows_here, width_here)
    )
    span_count = rows_here // SPAN
    entries = neighbours[0].reshape(-1)
    per_owner = database.shape[1]
    owner_count = lax.axis_size("db")
    slot_count = entries.shape[0] // 2
    owner_of = entries // per_owner
    local_of = entries % per_owner
    owner_hits = (owner_of[:, None] == jnp.arange(owner_count, dtype=jnp.int32)[None, :]).astype(
        jnp.int32
    )
    rank_of = jnp.sum((jnp.cumsum(owner_hits, axis=0) - owner_hits) * owner_hits, axis=1)
    place_of = owner_of * slot_count + rank_of
    place_hits = (
        place_of[:, None] == jnp.arange(owner_count * slot_count, dtype=jnp.int32)[None, :]
    ).astype(jnp.int32)
    request = jnp.sum(place_hits * local_of[:, None], axis=0).reshape(owner_count, slot_count)
    asked = lax.all_to_all(request, "db", split_axis=0, concat_axis=0, tiled=True)
    fetched = jnp.take(database, asked.reshape(-1), axis=1).reshape(
        2, owner_count, slot_count, database.shape[2], width_here
    )
    returned = lax.all_to_all(fetched, "db", split_axis=1, concat_axis=1, tiled=True)
    flat_rows = returned.reshape(2, owner_count * slot_count, database.shape[2], width_here)
    near_rows = jnp.take(flat_rows, place_of, axis=1).reshape(2, span_count, -1, head_count, DH)
    cross_heads = cross_queries[0].reshape(span_count, SPAN, head_count, DH)
    cross_score = (
        jnp.einsum("cqhd,ckhd->chqk", cross_heads, near_rows[0], preferred_element_type=jnp.float32)
        * scale
    )
    cross_peak = jnp.max(cross_score, axis=-1)
    cross_weights = jnp.exp(cross_score - cross_peak[..., None])
    cross_total = jnp.sum(cross_weights, axis=-1)
    cross_accum = jnp.einsum(
        "chqk,ckhd->cqhd",
        cross_weights.astype(jnp.bfloat16),
        near_rows[1],
        preferred_element_type=jnp.float32,
    )
    cross_out = (
        (cross_accum / cross_total.transpose(0, 2, 1)[..., None])
        .astype(jnp.bfloat16)
        .reshape(rows_here, width_here)
    )
    terms = jnp.dot(
        cross_out,
        lax.all_gather(out_weight, "db", axis=1, tiled=True),
        preferred_element_type=jnp.float32,
    )
    summed = lax.psum_scatter(
        terms.astype(jnp.bfloat16), "tp", scatter_dimension=1, tiled=True
    ).astype(jnp.float32)
    mixed = (
        (hidden_in[0].astype(jnp.float32) + summed)
        .astype(jnp.bfloat16)
        .reshape(1, rows_here, width_here)
    )
    return (attended, mixed)


def solution(mesh):
    in_specs = (
        P("db", "ctx", "tp"),
        P("db", "ctx", "tp"),
        P("db", "ctx", "tp"),
        P("db", "ctx", "tp"),
        P("db", "ctx", "tp"),
        P("db", "ctx", None),
        P(None, "db", None, "tp"),
        P("tp", "db"),
    )
    out_specs = (P("db", "ctx", "tp"), P("db", "ctx", "tp"))
    return jax.shard_map(shards, mesh=mesh, in_specs=in_specs, out_specs=out_specs, check_vma=False)
```

profile of v0, /device:TPU:36, one launch (start us, length us, event | category | flops | bytes accessed | tf_op | source)
XLA Modules:
  0.0 442.6 jit_solution(12731190402128268232)
XLA Ops:
  8.6 12.6 %all_to_all.14 = s32[4,1,4]{2,1,0:T(1,128)S(1)} all-to-all(s32[4,1,4]{2,1,0:T(1,128)S(1)} %bitcast.96), channel_id=1, replica_groups=mesh['ctx'=16,'db'=4,'tp'=8] {'db'}, dimensions={0} | all-to-all | bytes 128 | tf_op jit(solution)/shard_map/all_to_all | solution.py:98
  22.5 2.7 gather_fusion
  25.2 2.6 copy.125
  28.4 2.4 copy.126
  30.8 5.0 %all-to-all-start.1 = ((bf16[2,4,4,128,512]{4,3,2,0,1:T(8,128)(2,1)}), bf16[2,4,4,128,512]{4,3,2,0,1:T(8,128)(2,1)}, u32[]{:S(2)}, u32[]{:S(2)}) async-start(bf16[2,4,4,128,512]{4,3,2,0,1:T(8,128)(2,1)} %copy.126), calls=%async_computation.1 | async-start | bytes 8388608 | tf_op jit(solution)/shard_map/all_to_all | solution.py:102
  40.1 155.1 %all-to-all-done.1 = bf16[2,4,4,128,512]{4,3,2,0,1:T(8,128)(2,1)} async-done(((bf16[2,4,4,128,512]{4,3,2,0,1:T(8,128)(2,1)}), bf16[2,4,4,128,512]{4,3,2,0,1:T(8,128)(2,1)}, u32[]{:S(2)}, u32[]{:S(2)}) %all-to-all-start.1) | async-done | bytes 4194336 | tf_op jit(solution)/shard_map/all_to_all | solution.py:102
  195.3 4.6 %copy.127 = bf16[2,4,4,128,512]{4,3,2,1,0:T(8,128)(2,1)} copy(bf16[2,4,4,128,512]{4,3,2,0,1:T(8,128)(2,1)} %all-to-all-done.1) | data formatting | bytes 8388608 | tf_op jit(solution)/shard_map/all_to_all | solution.py:102
  199.9 4.2 gather_fusion.1
  208.8 2.2 squeeze.35
  213.9 4.8 %convolution_convert_fusion = bf16[256,4096]{1,0:T(8,128)(2,1)} fusion(bf16[512,4096]{1,0:T(8,128)(2,1)} %all-gather.2.cloned.1.call-done, bf16[32,8,4,128]{3,2,1,0:T(4,128)(2,1)S(1)} %bitcast.93), kind=kOutput, calls=%fused_computation.26 | convolution fusion | flops 1074790400 | bytes 6553600 | tf_op jit(solution)/shard_map/dot_general | solution.py:124
  218.7 208.3 %while.22 = (s32[]{:T(128)}, bf16[2,4,256,128]{3,2,1,0:T(8,128)(2,1)}, f32[4,256]{1,0:T(4,128)S(1)}, f32[4,256]{1,0:T(4,128)S(1)}, f32[4,256,128]{2,1,0:T(8,128)...) while((s32[]{:T(128)}, ...), condition=%wide.region_3.4_spmd.clone, body=%wide.region_0.3_spmd.clone.sunk | while | flops 137041424 | bytes 8458558 | solution.py:60
  218.7 1.9 copy.158
  220.6 1.9 collective-permute-start
  224.3 2.2 convolution_add_fusion.3
  226.5 6.1 %collective-permute-done = bf16[2,4,256,128]{3,2,1,0:T(8,128)(2,1)} collective-permute-done((bf16[2,4,256,128]{3,2,1,0:T(8,128)(2,1)}, bf16[2,4,256,128]{3,2,1,0:T(8,128)(2,1)}, u32[]{:S(2)}, u32[]{:S(2)}) %collective-permute-start) | collective-permute-done | bytes 524320 | tf_op jit(solution)/shard_map/while/body/eval_jaxpr/ppermute | solution.py:15
  232.6 1.9 copy.158
  234.5 1.9 collective-permute-start
  238.2 2.4 convolution_add_fusion.3
  240.6 5.9 %collective-permute-done = bf16[2,4,256,128]{3,2,1,0:T(8,128)(2,1)} collective-permute-done((bf16[2,4,256,128]{3,2,1,0:T(8,128)(2,1)}, bf16[2,4,256,128]{3,2,1,0:T(8,128)(2,1)}, u32[]{:S(2)}, u32[]{:S(2)}) %collective-permute-start) | collective-permute-done | bytes 524320 | tf_op jit(solution)/shard_map/while/body/eval_jaxpr/ppermute | solution.py:15
  248.4 1.9 collective-permute-start
  252.1 2.4 convolution_add_fusion.3
  254.5 5.9 %collective-permute-done = bf16[2,4,256,128]{3,2,1,0:T(8,128)(2,1)} collective-permute-done((bf16[2,4,256,128]{3,2,1,0:T(8,128)(2,1)}, bf16[2,4,256,128]{3,2,1,0:T(8,128)(2,1)}, u32[]{:S(2)}, u32[]{:S(2)}) %collective-permute-start) | collective-permute-done | bytes 524320 | tf_op jit(solution)/shard_map/while/body/eval_jaxpr/ppermute | solution.py:15
  260.4 1.9 copy.158
  262.3 1.9 collective-permute-start
  266.0 2.4 convolution_add_fusion.3
  268.4 5.9 %collective-permute-done = bf16[2,4,256,128]{3,2,1,0:T(8,128)(2,1)} collective-permute-done((bf16[2,4,256,128]{3,2,1,0:T(8,128)(2,1)}, bf16[2,4,256,128]{3,2,1,0:T(8,128)(2,1)}, u32[]{:S(2)}, u32[]{:S(2)}) %collective-permute-start) | collective-permute-done | bytes 524320 | tf_op jit(solution)/shard_map/while/body/eval_jaxpr/ppermute | solution.py:15
  274.3 1.9 copy.158
  276.2 1.9 collective-permute-start
  279.9 2.4 convolution_add_fusion.3
  282.3 5.9 %collective-permute-done = bf16[2,4,256,128]{3,2,1,0:T(8,128)(2,1)} collective-permute-done((bf16[2,4,256,128]{3,2,1,0:T(8,128)(2,1)}, bf16[2,4,256,128]{3,2,1,0:T(8,128)(2,1)}, u32[]{:S(2)}, u32[]{:S(2)}) %collective-permute-start) | collective-permute-done | bytes 524320 | tf_op jit(solution)/shard_map/while/body/eval_jaxpr/ppermute | solution.py:15
  290.0 1.9 collective-permute-start
  293.7 2.4 convolution_add_fusion.3
  296.1 5.9 %collective-permute-done = bf16[2,4,256,128]{3,2,1,0:T(8,128)(2,1)} collective-permute-done((bf16[2,4,256,128]{3,2,1,0:T(8,128)(2,1)}, bf16[2,4,256,128]{3,2,1,0:T(8,128)(2,1)}, u32[]{:S(2)}, u32[]{:S(2)}) %collective-permute-start) | collective-permute-done | bytes 524320 | tf_op jit(solution)/shard_map/while/body/eval_jaxpr/ppermute | solution.py:15
  303.9 1.9 collective-permute-start
  307.6 2.4 convolution_add_fusion.3
  310.0 5.9 %collective-permute-done = bf16[2,4,256,128]{3,2,1,0:T(8,128)(2,1)} collective-permute-done((bf16[2,4,256,128]{3,2,1,0:T(8,128)(2,1)}, bf16[2,4,256,128]{3,2,1,0:T(8,128)(2,1)}, u32[]{:S(2)}, u32[]{:S(2)}) %collective-permute-start) | collective-permute-done | bytes 524320 | tf_op jit(solution)/shard_map/while/body/eval_jaxpr/ppermute | solution.py:15
  317.8 1.9 collective-permute-start
  321.5 2.4 convolution_add_fusion.3
  323.9 5.9 %collective-permute-done = bf16[2,4,256,128]{3,2,1,0:T(8,128)(2,1)} collective-permute-done((bf16[2,4,256,128]{3,2,1,0:T(8,128)(2,1)}, bf16[2,4,256,128]{3,2,1,0:T(8,128)(2,1)}, u32[]{:S(2)}, u32[]{:S(2)}) %collective-permute-start) | collective-permute-done | bytes 524320 | tf_op jit(solution)/shard_map/while/body/eval_jaxpr/ppermute | solution.py:15
  329.8 1.9 copy.158
  331.7 1.9 collective-permute-start
  335.4 2.4 convolution_add_fusion.3
  337.8 5.9 %collective-permute-done = bf16[2,4,256,128]{3,2,1,0:T(8,128)(2,1)} collective-permute-done((bf16[2,4,256,128]{3,2,1,0:T(8,128)(2,1)}, bf16[2,4,256,128]{3,2,1,0:T(8,128)(2,1)}, u32[]{:S(2)}, u32[]{:S(2)}) %collective-permute-start) | collective-permute-done | bytes 524320 | tf_op jit(solution)/shard_map/while/body/eval_jaxpr/ppermute | solution.py:15
  343.7 1.9 copy.158
  345.6 1.9 collective-permute-start
  349.3 2.4 convolution_add_fusion.3
  351.7 5.9 %collective-permute-done = bf16[2,4,256,128]{3,2,1,0:T(8,128)(2,1)} collective-permute-done((bf16[2,4,256,128]{3,2,1,0:T(8,128)(2,1)}, bf16[2,4,256,128]{3,2,1,0:T(8,128)(2,1)}, u32[]{:S(2)}, u32[]{:S(2)}) %collective-permute-start) | collective-permute-done | bytes 524320 | tf_op jit(solution)/shard_map/while/body/eval_jaxpr/ppermute | solution.py:15
  359.5 1.9 collective-permute-start
  363.2 2.4 convolution_add_fusion.3
  365.6 5.9 %collective-permute-done = bf16[2,4,256,128]{3,2,1,0:T(8,128)(2,1)} collective-permute-done((bf16[2,4,256,128]{3,2,1,0:T(8,128)(2,1)}, bf16[2,4,256,128]{3,2,1,0:T(8,128)(2,1)}, u32[]{:S(2)}, u32[]{:S(2)}) %collective-permute-start) | collective-permute-done | bytes 524320 | tf_op jit(solution)/shard_map/while/body/eval_jaxpr/ppermute | solution.py:15
  373.3 1.9 collective-permute-start
  377.0 2.4 convolution_add_fusion.3
  379.4 5.9 %collective-permute-done = bf16[2,4,256,128]{3,2,1,0:T(8,128)(2,1)} collective-permute-done((bf16[2,4,256,128]{3,2,1,0:T(8,128)(2,1)}, bf16[2,4,256,128]{3,2,1,0:T(8,128)(2,1)}, u32[]{:S(2)}, u32[]{:S(2)}) %collective-permute-start) | collective-permute-done | bytes 524320 | tf_op jit(solution)/shard_map/while/body/eval_jaxpr/ppermute | solution.py:15
  385.4 1.9 copy.158
  387.2 1.9 collective-permute-start
  390.9 2.4 convolution_add_fusion.3
  393.3 5.9 %collective-permute-done = bf16[2,4,256,128]{3,2,1,0:T(8,128)(2,1)} collective-permute-done((bf16[2,4,256,128]{3,2,1,0:T(8,128)(2,1)}, bf16[2,4,256,128]{3,2,1,0:T(8,128)(2,1)}, u32[]{:S(2)}, u32[]{:S(2)}) %collective-permute-start) | collective-permute-done | bytes 524320 | tf_op jit(solution)/shard_map/while/body/eval_jaxpr/ppermute | solution.py:15
  399.2 1.9 copy.158
  401.1 1.9 collective-permute-start
  404.8 2.4 convolution_add_fusion.3
  407.2 5.9 %collective-permute-done = bf16[2,4,256,128]{3,2,1,0:T(8,128)(2,1)} collective-permute-done((bf16[2,4,256,128]{3,2,1,0:T(8,128)(2,1)}, bf16[2,4,256,128]{3,2,1,0:T(8,128)(2,1)}, u32[]{:S(2)}, u32[]{:S(2)}) %collective-permute-start) | collective-permute-done | bytes 524320 | tf_op jit(solution)/shard_map/while/body/eval_jaxpr/ppermute | solution.py:15
  415.0 1.9 collective-permute-start
  418.7 2.4 convolution_add_fusion.3
  421.1 5.9 %collective-permute-done = bf16[2,4,256,128]{3,2,1,0:T(8,128)(2,1)} collective-permute-done((bf16[2,4,256,128]{3,2,1,0:T(8,128)(2,1)}, bf16[2,4,256,128]{3,2,1,0:T(8,128)(2,1)}, u32[]{:S(2)}, u32[]{:S(2)}) %collective-permute-start) | collective-permute-done | bytes 524320 | tf_op jit(solution)/shard_map/while/body/eval_jaxpr/ppermute | solution.py:15
  (194 shorter events, 62.3 us)
Async XLA Ops:
  7.2 15.3 %copy-start = (bf16[2,8,128,512]{3,2,1,0:T(8,128)(2,1)S(1)}, bf16[2,8,128,512]{3,2,1,0:T(8,128)(2,1)}, u32[]{:S(2)}) copy-start(bf16[2,8,128,512]{3,2,1,0:T(8,128)(2,1)} %param.16) | copy-start | bytes 6291460
  30.8 5.9 %copy-start.4 = (bf16[1,256,512]{2,1,0:T(8,128)(2,1)S(1)}, bf16[1,256,512]{2,1,0:T(8,128)(2,1)}, u32[]{:S(2)}) copy-start(bf16[1,256,512]{2,1,0:T(8,128)(2,1)} %param.14) | copy-start | bytes 786436
  30.8 5.9 %copy-start.5 = (bf16[1,256,512]{2,1,0:T(8,128)(2,1)S(1)}, bf16[1,256,512]{2,1,0:T(8,128)(2,1)}, u32[]{:S(2)}) copy-start(bf16[1,256,512]{2,1,0:T(8,128)(2,1)} %param.11) | copy-start | bytes 786436
  30.8 6.9 %copy-start.6 = (bf16[1,256,512]{2,1,0:T(8,128)(2,1)S(1)}, bf16[1,256,512]{2,1,0:T(8,128)(2,1)}, u32[]{:S(2)}) copy-start(bf16[1,256,512]{2,1,0:T(8,128)(2,1)} %param.12) | copy-start | bytes 786436
  30.8 164.4 %all-to-all-start.1 = ((bf16[2,4,4,128,512]{4,3,2,0,1:T(8,128)(2,1)}), bf16[2,4,4,128,512]{4,3,2,0,1:T(8,128)(2,1)}, u32[]{:S(2)}, u32[]{:S(2)}) async-start(bf16[2,4,4,128,512]{4,3,2,0,1:T(8,128)(2,1)} %copy.126), calls=%async_computation.1 | async-start | bytes 8388608 | tf_op jit(solution)/shard_map/all_to_all | solution.py:102
  35.8 178.1 %all-gather.2.cloned.1.call-start = ((), (), s32[]{:S(2)}) async-start(), calls=%async_computation.3 | async-start | bytes 5242880 | tf_op jit(solution)/shard_map/all_gather | solution.py:126
  36.5 397.5 %reduce-scatter.2.cloned.1.call-start = ((), (), s32[]{:S(2)}) async-start(), calls=%async_computation.4 | async-start | bytes 2359296 | tf_op jit(solution)/shard_map/reduce_scatter | solution.py:129
  36.9 2.1 copy-start.1
  218.7 211.0 %copy-start.2 = (bf16[1,256,512]{1,2,0:T(8,128)(2,1)S(1)}, bf16[1,256,512]{1,2,0:T(8,128)(2,1)}, u32[]{:S(2)}) copy-start(bf16[1,256,512]{1,2,0:T(8,128)(2,1)} %copy-done.1) | copy-start | bytes 786436
  220.6 12.0 %collective-permute-start = (bf16[2,4,256,128]{3,2,1,0:T(8,128)(2,1)}, bf16[2,4,256,128]{3,2,1,0:T(8,128)(2,1)}, u32[]{:S(2)}, u32[]{:S(2)}) collective-permute-start(bf16[2,4,256,128]{3,2,1,0:T(8,128)(2,1)} %copy.158), channel_id=1, source_target_pairs={{0,32},{32,64},{64,96},{96,128},{128,160},{160,192},{192,224},{224... | collective-permute-start | bytes 1572872 | tf_op jit(solution)/shard_map/while/body/eval_jaxpr/ppermute | solution.py:15
  234.5 12.0 %collective-permute-start = (bf16[2,4,256,128]{3,2,1,0:T(8,128)(2,1)}, bf16[2,4,256,128]{3,2,1,0:T(8,128)(2,1)}, u32[]{:S(2)}, u32[]{:S(2)}) collective-permute-start(bf16[2,4,256,128]{3,2,1,0:T(8,128)(2,1)} %copy.158), channel_id=1, source_target_pairs={{0,32},{32,64},{64,96},{96,128},{128,160},{160,192},{192,224},{224... | collective-permute-start | bytes 1572872 | tf_op jit(solution)/shard_map/while/body/eval_jaxpr/ppermute | solution.py:15
  248.4 12.0 %collective-permute-start = (bf16[2,4,256,128]{3,2,1,0:T(8,128)(2,1)}, bf16[2,4,256,128]{3,2,1,0:T(8,128)(2,1)}, u32[]{:S(2)}, u32[]{:S(2)}) collective-permute-start(bf16[2,4,256,128]{3,2,1,0:T(8,128)(2,1)} %copy.158), channel_id=1, source_target_pairs={{0,32},{32,64},{64,96},{96,128},{128,160},{160,192},{192,224},{224... | collective-permute-start | bytes 1572872 | tf_op jit(solution)/shard_map/while/body/eval_jaxpr/ppermute | solution.py:15
  262.3 12.0 %collective-permute-start = (bf16[2,4,256,128]{3,2,1,0:T(8,128)(2,1)}, bf16[2,4,256,128]{3,2,1,0:T(8,128)(2,1)}, u32[]{:S(2)}, u32[]{:S(2)}) collective-permute-start(bf16[2,4,256,128]{3,2,1,0:T(8,128)(2,1)} %copy.158), channel_id=1, source_target_pairs={{0,32},{32,64},{64,96},{96,128},{128,160},{160,192},{192,224},{224... | collective-permute-start | bytes 1572872 | tf_op jit(solution)/shard_map/while/body/eval_jaxpr/ppermute | solution.py:15
  276.2 12.0 %collective-permute-start = (bf16[2,4,256,128]{3,2,1,0:T(8,128)(2,1)}, bf16[2,4,256,128]{3,2,1,0:T(8,128)(2,1)}, u32[]{:S(2)}, u32[]{:S(2)}) collective-permute-start(bf16[2,4,256,128]{3,2,1,0:T(8,128)(2,1)} %copy.158), channel_id=1, source_target_pairs={{0,32},{32,64},{64,96},{96,128},{128,160},{160,192},{192,224},{224... | collective-permute-start | bytes 1572872 | tf_op jit(solution)/shard_map/while/body/eval_jaxpr/ppermute | solution.py:15
  290.0 12.0 %collective-permute-start = (bf16[2,4,256,128]{3,2,1,0:T(8,128)(2,1)}, bf16[2,4,256,128]{3,2,1,0:T(8,128)(2,1)}, u32[]{:S(2)}, u32[]{:S(2)}) collective-permute-start(bf16[2,4,256,128]{3,2,1,0:T(8,128)(2,1)} %copy.158), channel_id=1, source_target_pairs={{0,32},{32,64},{64,96},{96,128},{128,160},{160,192},{192,224},{224... | collective-permute-start | bytes 1572872 | tf_op jit(solution)/shard_map/while/body/eval_jaxpr/ppermute | solution.py:15
  303.9 12.0 %collective-permute-start = (bf16[2,4,256,128]{3,2,1,0:T(8,128)(2,1)}, bf16[2,4,256,128]{3,2,1,0:T(8,128)(2,1)}, u32[]{:S(2)}, u32[]{:S(2)}) collective-permute-start(bf16[2,4,256,128]{3,2,1,0:T(8,128)(2,1)} %copy.158), channel_id=1, source_target_pairs={{0,32},{32,64},{64,96},{96,128},{128,160},{160,192},{192,224},{224... | collective-permute-start | bytes 1572872 | tf_op jit(solution)/shard_map/while/body/eval_jaxpr/ppermute | solution.py:15
  317.8 12.0 %collective-permute-start = (bf16[2,4,256,128]{3,2,1,0:T(8,128)(2,1)}, bf16[2,4,256,128]{3,2,1,0:T(8,128)(2,1)}, u32[]{:S(2)}, u32[]{:S(2)}) collective-permute-start(bf16[2,4,256,128]{3,2,1,0:T(8,128)(2,1)} %copy.158), channel_id=1, source_target_pairs={{0,32},{32,64},{64,96},{96,128},{128,160},{160,192},{192,224},{224... | collective-permute-start | bytes 1572872 | tf_op jit(solution)/shard_map/while/body/eval_jaxpr/ppermute | solution.py:15
  331.7 12.0 %collective-permute-start = (bf16[2,4,256,128]{3,2,1,0:T(8,128)(2,1)}, bf16[2,4,256,128]{3,2,1,0:T(8,128)(2,1)}, u32[]{:S(2)}, u32[]{:S(2)}) collective-permute-start(bf16[2,4,256,128]{3,2,1,0:T(8,128)(2,1)} %copy.158), channel_id=1, source_target_pairs={{0,32},{32,64},{64,96},{96,128},{128,160},{160,192},{192,224},{224... | collective-permute-start | bytes 1572872 | tf_op jit(solution)/shard_map/while/body/eval_jaxpr/ppermute | solution.py:15
  345.6 12.0 %collective-permute-start = (bf16[2,4,256,128]{3,2,1,0:T(8,128)(2,1)}, bf16[2,4,256,128]{3,2,1,0:T(8,128)(2,1)}, u32[]{:S(2)}, u32[]{:S(2)}) collective-permute-start(bf16[2,4,256,128]{3,2,1,0:T(8,128)(2,1)} %copy.158), channel_id=1, source_target_pairs={{0,32},{32,64},{64,96},{96,128},{128,160},{160,192},{192,224},{224... | collective-permute-start | bytes 1572872 | tf_op jit(solution)/shard_map/while/body/eval_jaxpr/ppermute | solution.py:15
  359.5 12.0 %collective-permute-start = (bf16[2,4,256,128]{3,2,1,0:T(8,128)(2,1)}, bf16[2,4,256,128]{3,2,1,0:T(8,128)(2,1)}, u32[]{:S(2)}, u32[]{:S(2)}) collective-permute-start(bf16[2,4,256,128]{3,2,1,0:T(8,128)(2,1)} %copy.158), channel_id=1, source_target_pairs={{0,32},{32,64},{64,96},{96,128},{128,160},{160,192},{192,224},{224... | collective-permute-start | bytes 1572872 | tf_op jit(solution)/shard_map/while/body/eval_jaxpr/ppermute | solution.py:15
  373.3 12.0 %collective-permute-start = (bf16[2,4,256,128]{3,2,1,0:T(8,128)(2,1)}, bf16[2,4,256,128]{3,2,1,0:T(8,128)(2,1)}, u32[]{:S(2)}, u32[]{:S(2)}) collective-permute-start(bf16[2,4,256,128]{3,2,1,0:T(8,128)(2,1)} %copy.158), channel_id=1, source_target_pairs={{0,32},{32,64},{64,96},{96,128},{128,160},{160,192},{192,224},{224... | collective-permute-start | bytes 1572872 | tf_op jit(solution)/shard_map/while/body/eval_jaxpr/ppermute | solution.py:15
  387.2 12.0 %collective-permute-start = (bf16[2,4,256,128]{3,2,1,0:T(8,128)(2,1)}, bf16[2,4,256,128]{3,2,1,0:T(8,128)(2,1)}, u32[]{:S(2)}, u32[]{:S(2)}) collective-permute-start(bf16[2,4,256,128]{3,2,1,0:T(8,128)(2,1)} %copy.158), channel_id=1, source_target_pairs={{0,32},{32,64},{64,96},{96,128},{128,160},{160,192},{192,224},{224... | collective-permute-start | bytes 1572872 | tf_op jit(solution)/shard_map/while/body/eval_jaxpr/ppermute | solution.py:15
  401.1 12.0 %collective-permute-start = (bf16[2,4,256,128]{3,2,1,0:T(8,128)(2,1)}, bf16[2,4,256,128]{3,2,1,0:T(8,128)(2,1)}, u32[]{:S(2)}, u32[]{:S(2)}) collective-permute-start(bf16[2,4,256,128]{3,2,1,0:T(8,128)(2,1)} %copy.158), channel_id=1, source_target_pairs={{0,32},{32,64},{64,96},{96,128},{128,160},{160,192},{192,224},{224... | collective-permute-start | bytes 1572872 | tf_op jit(solution)/shard_map/while/body/eval_jaxpr/ppermute | solution.py:15
  415.0 12.0 %collective-permute-start = (bf16[2,4,256,128]{3,2,1,0:T(8,128)(2,1)}, bf16[2,4,256,128]{3,2,1,0:T(8,128)(2,1)}, u32[]{:S(2)}, u32[]{:S(2)}) collective-permute-start(bf16[2,4,256,128]{3,2,1,0:T(8,128)(2,1)} %copy.158), channel_id=1, source_target_pairs={{0,32},{32,64},{64,96},{96,128},{128,160},{160,192},{192,224},{224... | collective-permute-start | bytes 1572872 | tf_op jit(solution)/shard_map/while/body/eval_jaxpr/ppermute | solution.py:15
  430.9 3.1 copy-start.3
Sparse Core Ops, SparseCore 0:
  38.7 132.6 all-gather.1
  218.8 101.5 reduce-scatter.1
where the time goes:
time: 445 us; the launch traced here: 443 us
  waiting for transfers between devices  245 us (55%)
  matrix products  65.5 us (15%)
  local copies, waits for them, and re-layouts  59.4 us (13%)
  starting transfers between devices  33.7 us (8%)
  between operations  14.3 us (3%)
  blocking collectives  12.6 us (3%)
  other arithmetic  11.1 us (2%)
    all_to_all x1, waiting for transfers between devices, shards(): lax.all_to_all(fetched, 'db', split_axis=1, concat_axis=1, tiled=True)  155 us
    ppermute x15, waiting for transfers between devices, passed_along(): lax.ppermute(value, axis, [(source, source + steps) for source in range(l...  88.9 us
    dot_general x16, matrix products, absorb(): jnp.einsum('hqk,hkd->hqd', weights.astype(jnp.bfloat16), moving[1], prefe...  37 us
    ppermute x15, starting transfers between devices, passed_along(): lax.ppermute(value, axis, [(source, source + steps) for source in range(l...  28.6 us
    while x30, local copies, waits for them, and re-layouts  28.1 us
    dot_general x16, matrix products, absorb(): jnp.einsum('hqd,hkd->hqk', query_part, moving[0], preferred_element_type=...  21.6 us
    all_to_all x1, blocking collectives, shards(): lax.all_to_all(request, 'db', split_axis=0, concat_axis=0, tiled=True)  12.6 us
  transfers between devices with their start and end apart: 18, of which 16 were waited for; matrix products, arithmetic and copies ran while one was open for 27% of the time, Pallas kernels for 0%

commit v1 on v0

v1 whole, which is shorter than its diff:
```python
import functools
import math

import jax
import jax.numpy as jnp
from jax import lax
from jax.experimental import pallas as pl
from jax.experimental.pallas import tpu as pltpu
from jax.sharding import PartitionSpec as P

DH = 128
SPAN = 64
NEIGH = 2
SLOTS = 4
PER_SHARD = 8
ROW_BLOCKS = 2
MESH = pl.DeviceIdType.MESH
SCALE = 1.0 / math.sqrt(DH)
SCALE2 = SCALE * math.log2(math.e)
LOG2E = math.log2(math.e)
NT = (((1,), (1,)), ((), ()))


def remote(src, dst, send_sem, recv_sem, **where):
    return pltpu.make_async_remote_copy(
        src_ref=src, dst_ref=dst, send_sem=send_sem, recv_sem=recv_sem, device_id=where, device_id_type=MESH
    )


def layer(sizes, near_ref, hid_hbm, q_hbm, k_hbm, v_hbm, cq_hbm, db_hbm, w_hbm, att_ref, mixed_ref, *scratch):
    n_y, n_d, n_x = sizes
    half = n_y // 2
    (kv, qv, hid, nbv, nbs, tab, dbv, wg, osend, orecv, stf, stsend, strecv, stat, co, terms, xsend, xrecv,
     mine, zsend, zrecv, mref, lref, acc,
     loc_sem, ps, pr, ms, mr, cs, cr, qs, qr, ns, nr, nl, os_, or_, ss, sr, wzs, wzr, wps, wpr, wms, wmr, wcs, wcr,
     xs, xr, zs, zr) = scratch[n_d:]
    cqa = scratch[:n_d]
    rows = qv.shape[0]
    width = qv.shape[1]
    heads = width // DH
    spans = rows // SPAN
    entries = spans * NEIGH

    i = lax.axis_index("ctx")
    d = lax.axis_index("db")
    t = lax.axis_index("tp")
    y, c = i // 2, i % 2
    x, zh = t // 2, t % 2
    other = i + 1 - 2 * c
    up = (i + 2) % (2 * n_y)
    down = (i + 2 * n_y - 2) % (2 * n_y)
    right = ((x + 1) % n_x) * 2 + zh
    left = ((x + n_x - 1) % n_x) * 2 + zh
    across = x * 2 + 1 - zh

    loads = [
        (q_hbm, qv), (k_hbm, kv.at[i, 0]), (v_hbm, kv.at[i, 1]), (cq_hbm, cqa[0]),
        (db_hbm, dbv), (w_hbm, wg.at[:, 0]), (hid_hbm, hid),
    ]
    local = [pltpu.make_async_copy(a, b, loc_sem.at[n]) for n, (a, b) in enumerate(loads)]
    for copy in local:
        copy.start()

    lane = lax.broadcasted_iota(jnp.int32, (8, 128), 1)
    ids = jnp.zeros((8, 128), jnp.int32)
    for n in range(entries):
        ids = jnp.where(lane == n, near_ref[n // NEIGH, n % NEIGH], ids)
    nbv[0] = ids

    barrier = pltpu.get_barrier_semaphore()
    greet = [dict(ctx=up), dict(ctx=down), dict(ctx=other), dict(tp=right), dict(tp=left), dict(tp=across)]
    greet += [dict(db=(d + m) % n_d) for m in range(1, n_d)]
    for where in greet:
        pl.semaphore_signal(barrier, inc=1, device_id=where, device_id_type=MESH)
    pl.semaphore_wait(barrier, len(greet))

    def id_copy(m):
        return remote(nbv.at[0], nbv.at[n_d - m], ns.at[n_d - m], nr.at[n_d - m], db=(d + m) % n_d)

    def query_copy(m):
        return remote(cq_hbm, cqa[n_d - m], qs.at[n_d - m], qr.at[n_d - m], db=(d + m) % n_d)

    def weight_copy(m):
        j = n_d - m
        return remote(w_hbm.at[i], wg.at[i, j], wzs.at[j], wzr.at[j], db=(d + m) % n_d)

    def plus_has(step, part):
        return step < half - 1 or part == 0

    def plus_copy(step, part):
        slot = 2 * (y - step) + c
        src = (k_hbm, v_hbm)[part] if step == 0 else kv.at[slot, part]
        return remote(src, kv.at[slot, part], ps.at[step, part], pr.at[step, part], ctx=up)

    def minus_has(step, part):
        return part == 1 or step <= half - 2

    def minus_good(source, part):
        return source <= (half - 1 if part == 1 else half - 2)

    def minus_copy(step, part):
        slot = 2 * ((y + step) % n_y) + c
        src = (k_hbm, v_hbm)[part] if step == 0 else kv.at[slot, part]
        return remote(src, kv.at[slot, part], ms.at[step, part], mr.at[step, part], ctx=down)

    def pass_copy(source, part, own):
        slot = 2 * source + c
        src = (k_hbm, v_hbm)[part] if own else kv.at[slot, part]
        return remote(src, kv.at[slot, part], cs.at[source, part], cr.at[source, part], ctx=other)

    for m in range(1, n_d):
        id_copy(m).start()
    for m in range(1, n_d):
        query_copy(m).start()
    for part in (0, 1):
        if plus_has(0, part):
            pl.when(y < n_y - 1)(lambda part=part: plus_copy(0, part).start())
        if minus_has(0, part):
            pl.when(minus_good(y, part))(lambda part=part: minus_copy(0, part).start())
        pl.when(c == 0)(lambda part=part: pass_copy(y, part, True).start())
    for m in range(1, n_d):
        weight_copy(m).start()

    def attend_first():
        row = lax.broadcasted_iota(jnp.int32, (rows, rows), 0)
        col = lax.broadcasted_iota(jnp.int32, (rows, rows), 1)
        keep = col <= row
        for h in range(heads):
            hs = slice(h * DH, (h + 1) * DH)
            s = lax.dot_general(qv[:, hs], kv[i, 0, :, hs], NT, preferred_element_type=jnp.float32)
            s = jnp.where(keep, s, -1e30)
            peak = jnp.max(s, axis=-1, keepdims=True)
            p = jnp.exp2((s - peak) * SCALE2)
            mref[h] = peak
            lref[h] = jnp.sum(p, axis=-1, keepdims=True)
            acc[h] = jnp.dot(p.astype(jnp.bfloat16), kv[i, 1, :, hs], preferred_element_type=jnp.float32)

    def attend(start, count):
        for h in range(heads):
            hs = slice(h * DH, (h + 1) * DH)
            keys = kv[pl.ds(start, count), 0, :, hs].reshape(count * rows, DH)
            vals = kv[pl.ds(start, count), 1, :, hs].reshape(count * rows, DH)
            s = lax.dot_general(qv[:, hs], keys, NT, preferred_element_type=jnp.float32)
            before = mref[h]
            peak = jnp.maximum(before, jnp.max(s, axis=-1, keepdims=True))
            p = jnp.exp2((s - peak) * SCALE2)
            factor = jnp.exp2((before - peak) * SCALE2)
            mref[h] = peak
            lref[h] = lref[h] * factor + jnp.sum(p, axis=-1, keepdims=True)
            acc[h] = acc[h] * factor + jnp.dot(p.astype(jnp.bfloat16), vals, preferred_element_type=jnp.float32)

    def wait_passed(source):
        for part in (0, 1):
            slot = 2 * source + 1 - c
            remote(
                kv.at[slot, part], kv.at[slot, part], cs.at[source, part], cr.at[source, part], ctx=other
            ).wait_recv()

    def attend_pair(source):
        wait_passed(source)
        attend(2 * source, 2)

    def move_step(step):
        for part in (0, 1):
            if plus_has(step, part):
                source = y - 1 - step

                @pl.when(source >= 0)
                def _():
                    slot = 2 * source + c
                    remote(
                        kv.at[slot, part], kv.at[slot, part], ps.at[step, part], pr.at[step, part], ctx=up
                    ).wait_recv()
                    if step + 1 < half and plus_has(step + 1, part):
                        pl.when(y < n_y - 1)(lambda: plus_copy(step + 1, part).start())
                    pass_copy(source, part, False).start()

            if minus_has(step, part):
                source2 = (y + 1 + step) % n_y

                @pl.when(minus_good(source2, part))
                def _():
                    slot = 2 * source2 + c
                    remote(
                        kv.at[slot, part], kv.at[slot, part], ms.at[step, part], mr.at[step, part], ctx=down
                    ).wait_recv()
                    if step + 1 < half and minus_has(step + 1, part):
                        minus_copy(step + 1, part).start()
                    pl.when(source2 < y)(lambda: pass_copy(source2, part, False).start())

    def attend_step(step):
        if step < half - 1:
            pl.when(y - 1 - step >= 0)(lambda: attend_pair(y - 1 - step))
            pl.when(y + 1 + step >= n_y)(lambda: attend_pair(y + 1 + step - n_y))
        else:
            pl.when(y >= half)(lambda: attend_pair(y - half))

    def wplus(step):
        slot = 2 * ((y - step + n_y) % n_y) + c
        piece = wg.at[slot, pl.ds(1, n_d - 1)]
        return remote(piece, piece, wps.at[step], wpr.at[step], ctx=up)

    def wminus(step):
        slot = 2 * ((y + step) % n_y) + c
        piece = wg.at[slot, pl.ds(1, n_d - 1)]
        return remote(piece, piece, wms.at[step], wmr.at[step], ctx=down)

    def wpass(source):
        piece = wg.at[2 * source + c, pl.ds(1, n_d - 1)]
        return remote(piece, piece, wcs.at[source], wcr.at[source], ctx=other)

    def weight_step(step):
        if step == 0:
            for j in range(1, n_d):
                remote(w_hbm.at[i], wg.at[i, j], wzs.at[j], wzr.at[j], db=d).wait_recv()
            source = y
        else:
            source = (y - step + n_y) % n_y
            piece = wg.at[2 * source + c, pl.ds(1, n_d - 1)]
            remote(piece, piece, wps.at[step - 1], wpr.at[step - 1], ctx=up).wait_recv()
        if step < half:
            wplus(step).start()
        wpass(source).start()
        if step < half - 1 and step == 0:
            wminus(0).start()
        if 1 <= step <= half - 1:
            source2 = (y + step) % n_y
            piece2 = wg.at[2 * source2 + c, pl.ds(1, n_d - 1)]
            remote(piece2, piece2, wms.at[step - 1], wmr.at[step - 1], ctx=down).wait_recv()
            if step < half - 1:
                wminus(step).start()
            wpass(source2).start()

    def weight_ready():
        for source in range(n_y):
            piece = wg.at[2 * source + 1 - c, pl.ds(1, n_d - 1)]
            remote(piece, piece, wcs.at[source], wcr.at[source], ctx=other).wait_recv()

    def serve(j):
        if j > 0:
            remote(nbv.at[0], nbv.at[j], ns.at[j], nr.at[j], db=d).wait_recv()
        move = pltpu.make_async_copy(nbv.at[j], nbs.at[j], nl.at[j])
        move.start()
        move.wait()
        spots = [jnp.int32(0)] * SLOTS
        blocks = [jnp.int32(0)] * SLOTS
        seen = jnp.int32(0)
        for n in range(entries):
            block = nbs[j, 0, n]
            hit = (block // PER_SHARD) == d
            for k in range(SLOTS):
                take = jnp.logical_and(hit, seen == k)
                spots[k] = jnp.where(take, n // NEIGH, spots[k])
                blocks[k] = jnp.where(take, block % PER_SHARD, blocks[k])
            seen = seen + jnp.where(hit, 1, 0)
        for k in range(SLOTS):
            tab[0, k] = spots[k]
            tab[1, k] = blocks[k]
        if j > 0:
            remote(cq_hbm, cqa[j], qs.at[j], qr.at[j], db=d).wait_recv()

        def one(k, carry):
            query = cqa[j][tab[0, k]]
            keys = dbv[0, tab[1, k]]
            vals = dbv[1, tab[1, k]]
            lanes = lax.broadcasted_iota(jnp.int32, (SPAN, 128), 1)
            st = jnp.zeros((SPAN, 128), jnp.float32)
            for h in range(heads):
                hs = slice(h * DH, (h + 1) * DH)
                s = lax.dot_general(query[:, hs], keys[:, hs], NT, preferred_element_type=jnp.float32)
                peak = jnp.max(s, axis=-1, keepdims=True)
                p = jnp.exp2((s - peak) * SCALE2)
                total = jnp.sum(p, axis=-1, keepdims=True)
                o = jnp.dot(p.astype(jnp.bfloat16), vals[:, hs], preferred_element_type=jnp.float32) / total
                if j == 0:
                    orecv[0, k, :, hs] = o.astype(jnp.bfloat16)
                else:
                    osend[j - 1, k, :, hs] = o.astype(jnp.bfloat16)
                st = jnp.where(lanes == h, peak * SCALE + jnp.log(total), st)
            if j == 0:
                stat[0, k] = st
            else:
                stf[k] = st
            return carry

        lax.fori_loop(0, SLOTS, one, 0)
        if j > 0:
            stsend[j - 1] = stf[...].reshape(SLOTS * SPAN, 128).T[:8]
            out_copy(j).start()
            stat_copy(j).start()

    def out_copy(j):
        return remote(osend.at[j - 1], orecv.at[n_d - j], os_.at[n_d - j], or_.at[n_d - j], db=(d + j) % n_d)

    def stat_copy(j):
        return remote(stsend.at[j - 1], strecv.at[n_d - j], ss.at[n_d - j], sr.at[n_d - j], db=(d + j) % n_d)

    def collect(j):
        remote(osend.at[0], orecv.at[j], os_.at[j], or_.at[j], db=d).wait_recv()
        remote(stsend.at[0], strecv.at[j], ss.at[j], sr.at[j], db=d).wait_recv()
        wide = jnp.concatenate([strecv[j]] * 16, axis=0)
        stat[j] = wide.T.reshape(SLOTS, SPAN, 128)

    def combine():
        places = []
        owners = []
        for n in range(entries):
            owner = nbs[0, 0, n] // PER_SHARD
            rank = jnp.int32(0)
            for earlier in owners:
                rank = rank + jnp.where(earlier == owner, 1, 0)
            owners.append(owner)
            places.append(((owner - d + n_d) % n_d, jnp.minimum(rank, SLOTS - 1)))
        for u in range(spans):
            (oa, ka), (ob, kb) = places[2 * u], places[2 * u + 1]
            sa, sb = stat[oa, ka], stat[ob, kb]
            peak = jnp.maximum(sa, sb)
            ea = jnp.exp2((sa - peak) * LOG2E)
            eb = jnp.exp2((sb - peak) * LOG2E)
            inv = 1.0 / (ea + eb)
            ea, eb = ea * inv, eb * inv
            va, vb = orecv[oa, ka], orecv[ob, kb]
            for h in range(heads):
                hs = slice(h * DH, (h + 1) * DH)
                o = va[:, hs].astype(jnp.float32) * ea[:, h:h + 1] + vb[:, hs].astype(jnp.float32) * eb[:, h:h + 1]
                co[u * SPAN:(u + 1) * SPAN, hs] = o.astype(jnp.bfloat16)

    half_w = terms.shape[2]

    def project(rho, side):
        j = ((x + rho) % n_x - d + n_d) % n_d
        block = wg[:, j, :, side * half_w:(side + 1) * half_w].reshape(width, half_w)
        return jnp.dot(co[...], block, preferred_element_type=jnp.float32)

    rb_rows = rows // ROW_BLOCKS

    def ring_copy(side, step, rb):
        rs = pl.ds(rb * rb_rows, rb_rows)
        return remote(
            xsend.at[side, step, rs], xrecv.at[side, step, rs], xs.at[side, step, rb], xr.at[side, step, rb],
            tp=(right, left)[side],
        )

    def rho_of(side, step):
        return (n_x - 1 - step) % n_x if side == 0 else (1 + step) % n_x

    def ring_start():
        for side in (0, 1):
            xsend[side, 0] = project(rho_of(side, 0), side).astype(jnp.bfloat16)
            for rb in range(ROW_BLOCKS):
                ring_copy(side, 0, rb).start()
        for step in range(1, n_x):
            for side in (0, 1):
                terms[side * (n_x - 1) + step - 1] = project(rho_of(side, step), side)

    def ring_step(step):
        for rb in range(ROW_BLOCKS):
            rs = slice(rb * rb_rows, (rb + 1) * rb_rows)
            for side in (0, 1):
                ring_copy(side, step - 1, rb).wait_recv()
                total = xrecv[side, step - 1, rs].astype(jnp.float32) + terms[side * (n_x - 1) + step - 1, rs]
                xsend[side, step, rs] = total.astype(jnp.bfloat16)
                ring_copy(side, step, rb).start()

    def z_copy(rb):
        rs = pl.ds(rb * rb_rows, rb_rows)
        return remote(zsend.at[rs], zrecv.at[rs], zs.at[rb], zr.at[rb], tp=across)

    def ring_end():
        for rb in range(ROW_BLOCKS):
            rs = slice(rb * rb_rows, (rb + 1) * rb_rows)
            sums = []
            for side in (0, 1):
                ring_copy(side, n_x - 2, rb).wait_recv()
                sums.append(
                    xrecv[side, n_x - 2, rs].astype(jnp.float32) + terms[side * (n_x - 1) + n_x - 2, rs]
                )
            zsend[rs] = jnp.where(zh == 0, sums[1], sums[0]).astype(jnp.bfloat16)
            z_copy(rb).start()
            mine[rs] = jnp.where(zh == 0, sums[0], sums[1]) + hid[rs].astype(jnp.float32)

    def finish_self():
        for h in range(heads):
            hs = slice(h * DH, (h + 1) * DH)
            att_ref[:, hs] = (acc[h] / lref[h]).astype(jnp.bfloat16)

    for n in (3, 4):
        local[n].wait()
    serve(0)
    for n in (0, 1, 2):
        local[n].wait()
    attend_first()
    move_step(0)

    @pl.when(c == 1)
    def _():
        wait_passed(y)
        attend(i - 1, 1)

    for j in [v for v in (1, n_d - 1) if v < n_d]:
        if j == 1 or n_d > 2:
            serve(j)
    for j in range(2, n_d - 1):
        serve(j)
    weight_step(0)
    move_step(1) if half > 1 else None
    weight_step(1)
    attend_step(0)
    weight_step(2) if half >= 2 else None
    move_step(2) if half > 2 else None
    if half > 1:
        attend_step(1)
    for step in range(3, half + 1):
        weight_step(step)
    for j in range(1, n_d):
        collect(j)
    combine()
    weight_ready()
    local[5].wait()
    ring_start()
    if half > 3:
        move_step(3)
    for step in range(1, n_x - 1):
        ring_step(step)
        if step == 1 and half > 2:
            attend_step(2)
    local[6].wait()
    ring_end()
    if half > 3:
        attend_step(3)
    finish_self()
    for rb in range(ROW_BLOCKS):
        rs = slice(rb * rb_rows, (rb + 1) * rb_rows)
        z_copy(rb).wait_recv()
        mixed_ref[rs] = (mine[rs] + zrecv[rs].astype(jnp.float32)).astype(jnp.bfloat16)

    for m in range(1, n_d):
        id_copy(m).wait_send()
        query_copy(m).wait_send()
        weight_copy(m).wait_send()
        out_copy(m).wait_send()
        stat_copy(m).wait_send()
    for step in range(half):
        for part in (0, 1):
            if plus_has(step, part):
                pl.when(jnp.logical_and(y - step >= 0, y < n_y - 1))(
                    lambda step=step, part=part: plus_copy(step, part).wait_send())
            if minus_has(step, part):
                pl.when(minus_good((y + step) % n_y, part))(
                    lambda step=step, part=part: minus_copy(step, part).wait_send())
        wplus(step).wait_send()
        if step < half - 1:
            wminus(step).wait_send()
    for source in range(n_y):
        for part in (0, 1):
            pl.when(source < y)(lambda source=source, part=part: pass_copy(source, part, False).wait_send())
        wpass(source).wait_send()
    for part in (0, 1):
        pl.when(c == 0)(lambda part=part: pass_copy(y, part, True).wait_send())
    for side in (0, 1):
        for step in range(n_x - 1):
            for rb in range(ROW_BLOCKS):
                ring_copy(side, step, rb).wait_send()
    for rb in range(ROW_BLOCKS):
        z_copy(rb).wait_send()


def shards(sizes, hidden_in, queries, keys, values, cross_queries, neighbours, database, out_weight):
    n_y, n_d, n_x = sizes
    half = n_y // 2
    rows, width = queries.shape[1:]
    heads = width // DH
    spans = rows // SPAN
    n_c = 2 * n_y
    piece = width // n_c
    cols = out_weight.shape[1]
    half_w = cols // 2
    bf16, f32 = jnp.bfloat16, jnp.float32
    vm, dma = pltpu.VMEM, pltpu.SemaphoreType.DMA
    any_spec = pl.BlockSpec(memory_space=pl.ANY)
    scratch = [vm((spans, SPAN, width), bf16) for _ in range(n_d)] + [
        vm((n_c, 2, rows, width), bf16),
        vm((rows, width), bf16),
        vm((rows, width), bf16),
        vm((n_d, 8, 128), jnp.int32),
        pltpu.SMEM((n_d, 8, 128), jnp.int32),
        pltpu.SMEM((2, SLOTS), jnp.int32),
        vm(database.shape, bf16),
        vm((n_c, n_d, piece, cols), bf16),
        vm((max(n_d - 1, 1), SLOTS, SPAN, width), bf16),
        vm((n_d, SLOTS, SPAN, width), bf16),
        vm((SLOTS, SPAN, 128), f32),
        vm((max(n_d - 1, 1), 8, SLOTS * SPAN), f32),
        vm((n_d, 8, SLOTS * SPAN), f32),
        vm((n_d, SLOTS, SPAN, 128), f32),
        vm((rows, width), bf16),
        vm((2 * (n_x - 1), rows, half_w), f32),
        vm((2, n_x - 1, rows, half_w), bf16),
        vm((2, n_x - 1, rows, half_w), bf16),
        vm((rows, half_w), f32),
        vm((rows, half_w), bf16),
        vm((rows, half_w), bf16),
        vm((heads, rows, 1), f32),
        vm((heads, rows, 1), f32),
        vm((heads, rows, DH), f32),
        dma((7,)),
        dma((half, 2)), dma((half, 2)), dma((half, 2)), dma((half, 2)),
        dma((n_y, 2)), dma((n_y, 2)),
        dma((n_d,)), dma((n_d,)), dma((n_d,)), dma((n_d,)), dma((n_d,)),
        dma((n_d,)), dma((n_d,)), dma((n_d,)), dma((n_d,)),
        dma((n_d,)), dma((n_d,)),
        dma((half,)), dma((half,)), dma((half,)), dma((half,)),
        dma((n_y,)), dma((n_y,)),
        dma((2, n_x - 1, ROW_BLOCKS)), dma((2, n_x - 1, ROW_BLOCKS)),
        dma((ROW_BLOCKS,)), dma((ROW_BLOCKS,)),
    ]
    attended, mixed = pl.pallas_call(
        functools.partial(layer, sizes),
        out_shape=(
            jax.ShapeDtypeStruct((rows, width), bf16),
            jax.ShapeDtypeStruct((rows, half_w), bf16),
        ),
        in_specs=[pl.BlockSpec(memory_space=pltpu.SMEM)] + [any_spec] * 7,
        out_specs=(pl.BlockSpec(memory_space=pltpu.VMEM), pl.BlockSpec(memory_space=pltpu.VMEM)),
        scratch_shapes=scratch,
        compiler_params=pltpu.CompilerParams(
            collective_id=0, has_side_effects=True, vmem_limit_bytes=56 * 1024 * 1024
        ),
        name="layer",
    )(
        neighbours[0],
        hidden_in[0],
        queries[0],
        keys[0],
        values[0],
        cross_queries[0].reshape(spans, SPAN, width),
        database,
        out_weight.reshape(n_c, piece, cols),
    )
    return attended[None], mixed[None]


def solution(mesh):
    sizes = (mesh.shape["ctx"] // 2, mesh.shape["db"], mesh.shape["tp"] // 2)
    in_specs = (
        P("db", "ctx", "tp"),
        P("db", "ctx", "tp"),
        P("db", "ctx", "tp"),
        P("db", "ctx", "tp"),
        P("db", "ctx", "tp"),
        P("db", "ctx", None),
        P(None, "db", None, "tp"),
        P("tp", "db"),
    )
    out_specs = (P("db", "ctx", "tp"), P("db", "ctx", "tp"))
    return jax.shard_map(
        functools.partial(shards, sizes), mesh=mesh, in_specs=in_specs, out_specs=out_specs, check_vma=False
    )
```

time: 445 us -> 130 us (0.29)
  the two profiles are of different devices: /device:TPU:36 before, /device:TPU:112 now
where the time goes in v1:
time: 130 us; the launch traced here: 129 us
  Pallas kernels  124 us (95%)
  local copies, waits for them, and re-layouts  4.68 us (4%)
    pallas_call x1, Pallas kernels, shards(): pl.pallas_call(functools.partial(layer, sizes), out_shape=(jax.ShapeDtype...  124 us
    unnamed x2, local copies, waits for them, and re-layouts  3.34 us

profile of v1, /device:TPU:112, one launch (start us, length us, event | category | flops | bytes accessed | tf_op | source)
XLA Modules:
  0.0 129.4 jit_solution(4354905401620294716)
XLA Ops:
  0.6 1.3 %copy.10.near_ref = s32[4,2]{1,0:T(4,128)} copy(s32[4,2]{0,1:T(2,128)} %bitcast.17) | data formatting | bytes 64 | tf_op jit(solution)/shard_map/squeeze | solution.py:531
  2.0 124.1 %layer.1 = (bf16[256,512]{1,0:T(8,128)(2,1)}, bf16[256,512]{1,0:T(8,128)(2,1)}) custom-call(s32[4,2]{1,0:T(4,128)} %copy.10.near_ref, bf16[256,512]{1,0:T(8,128)(2,1)} %bitcast.10, bf16[256,512]{1,0:T(8,128)(2,1)} %bitcast.11, bf16[256,512]{1,0:T(8,128)(2,1)} %bitcast.12, bf16[256,512]{1,0:T(8,128)(2,1)} %bitcast.13, bf16[4,64,512]{2,1,0:T(8,128)(2,1)} %bitcast.14, ...), custom_call_target="tpu_custom_call" | custom-call | tf_op jit(solution)/shard_map/layer/pallas_call | solution.py:517
  126.1 1.7 %copy.13 = bf16[1,256,512]{2,1,0:T(8,128)(2,1)} copy(bf16[1,256,512]{2,1,0:T(8,128)(2,1)} %bitcast.16) | data formatting | bytes 524288
  127.7 1.7 %copy.14 = bf16[1,256,512]{2,1,0:T(8,128)(2,1)} copy(bf16[1,256,512]{2,1,0:T(8,128)(2,1)} %bitcast.15) | data formatting | bytes 524288

commit v2 on v1

--- a/solution.py
+++ b/solution.py
@@ -27,10 +27,10 @@
     )
 
 
-def layer(sizes, near_ref, hid_hbm, q_hbm, k_hbm, v_hbm, cq_hbm, db_hbm, w_hbm, att_ref, mixed_ref, *scratch):
+def layer(sizes, near_hbm, hid_hbm, q_hbm, k_hbm, v_hbm, cq_hbm, db_hbm, w_hbm, att_ref, mixed_ref, *scratch):
     n_y, n_d, n_x = sizes
     half = n_y // 2
-    (kv, qv, hid, nbv, nbs, tab, dbv, wg, osend, orecv, stf, stsend, strecv, stat, co, terms, xsend, xrecv,
+    (kv, qv, hid, near_ref, nbv, nbs, dbv, wg, osend, orecv, stsend, strecv, stat, co, terms, xsend, xrecv,
      mine, zsend, zrecv, mref, lref, acc,
      loc_sem, ps, pr, ms, mr, cs, cr, qs, qr, ns, nr, nl, os_, or_, ss, sr, wzs, wzr, wps, wpr, wms, wmr, wcs, wcr,
      xs, xr, zs, zr) = scratch[n_d:]
@@ -55,23 +55,23 @@
 
     loads = [
         (q_hbm, qv), (k_hbm, kv.at[i, 0]), (v_hbm, kv.at[i, 1]), (cq_hbm, cqa[0]),
-        (db_hbm, dbv), (w_hbm, wg.at[:, 0]), (hid_hbm, hid),
+        (db_hbm, dbv), (w_hbm, wg.at[:, 0]), (hid_hbm, hid), (near_hbm.at[0], near_ref),
     ]
     local = [pltpu.make_async_copy(a, b, loc_sem.at[n]) for n, (a, b) in enumerate(loads)]
-    for copy in local:
-        copy.start()
-
+    for n in (7, 3, 4, 0, 1, 2, 5, 6):
+        local[n].start()
+    barrier = pltpu.get_barrier_semaphore()
+    greet = [dict(ctx=up), dict(ctx=down), dict(ctx=other), dict(tp=right), dict(tp=left), dict(tp=across)]
+    greet += [dict(db=(d + m) % n_d) for m in range(1, n_d)]
+    for where in greet:
+        pl.semaphore_signal(barrier, inc=1, device_id=where, device_id_type=MESH)
+
+    local[7].wait()
     lane = lax.broadcasted_iota(jnp.int32, (8, 128), 1)
     ids = jnp.zeros((8, 128), jnp.int32)
     for n in range(entries):
         ids = jnp.where(lane == n, near_ref[n // NEIGH, n % NEIGH], ids)
     nbv[0] = ids
-
-    barrier = pltpu.get_barrier_semaphore()
-    greet = [dict(ctx=up), dict(ctx=down), dict(ctx=other), dict(tp=right), dict(tp=left), dict(tp=across)]
-    greet += [dict(db=(d + m) % n_d) for m in range(1, n_d)]
-    for where in greet:
-        pl.semaphore_signal(barrier, inc=1, device_id=where, device_id_type=MESH)
     pl.semaphore_wait(barrier, len(greet))
 
     def id_copy(m):
@@ -108,18 +108,18 @@
         src = (k_hbm, v_hbm)[part] if own else kv.at[slot, part]
         return remote(src, kv.at[slot, part], cs.at[source, part], cr.at[source, part], ctx=other)
 
+    def kv_start(part):
+        pl.when(y < n_y - 1)(lambda: plus_copy(0, part).start())
+        pl.when(minus_good(y, part))(lambda: minus_copy(0, part).start())
+        pl.when(c == 0)(lambda: pass_copy(y, part, True).start())
+
     for m in range(1, n_d):
         id_copy(m).start()
     for m in range(1, n_d):
+        weight_copy(m).start()
+    for m in range(1, n_d):
         query_copy(m).start()
-    for part in (0, 1):
-        if plus_has(0, part):
-            pl.when(y < n_y - 1)(lambda part=part: plus_copy(0, part).start())
-        if minus_has(0, part):
-            pl.when(minus_good(y, part))(lambda part=part: minus_copy(0, part).start())
-        pl.when(c == 0)(lambda part=part: pass_copy(y, part, True).start())
-    for m in range(1, n_d):
-        weight_copy(m).start()
+    kv_start(0)
 
     def attend_first():
         row = lax.broadcasted_iota(jnp.int32, (rows, rows), 0)
@@ -160,8 +160,8 @@
         wait_passed(source)
         attend(2 * source, 2)
 
-    def move_step(step):
-        for part in (0, 1):
+    def advance(step, *parts):
+        for part in parts:
             if plus_has(step, part):
                 source = y - 1 - step
 
@@ -236,56 +236,50 @@
             piece = wg.at[2 * source + 1 - c, pl.ds(1, n_d - 1)]
             remote(piece, piece, wcs.at[source], wcr.at[source], ctx=other).wait_recv()
 
-    def serve(j):
-        if j > 0:
-            remote(nbv.at[0], nbv.at[j], ns.at[j], nr.at[j], db=d).wait_recv()
-        move = pltpu.make_async_copy(nbv.at[j], nbs.at[j], nl.at[j])
-        move.start()
-        move.wait()
+    def id_move(j):
+        return pltpu.make_async_copy(nbv.at[j], nbs.at[j], nl.at[j])
+
+    def block_id(j, n):
+        return near_ref[n // NEIGH, n % NEIGH] if j == 0 else nbs[j, 0, n]
+
+    def lookups(j):
         spots = [jnp.int32(0)] * SLOTS
         blocks = [jnp.int32(0)] * SLOTS
         seen = jnp.int32(0)
         for n in range(entries):
-            block = nbs[j, 0, n]
+            block = block_id(j, n)
             hit = (block // PER_SHARD) == d
-            for k in range(SLOTS):
+            for k in range(min(n + 1, SLOTS)):
                 take = jnp.logical_and(hit, seen == k)
                 spots[k] = jnp.where(take, n // NEIGH, spots[k])
                 blocks[k] = jnp.where(take, block % PER_SHARD, blocks[k])
             seen = seen + jnp.where(hit, 1, 0)
-        for k in range(SLOTS):
-            tab[0, k] = spots[k]
-            tab[1, k] = blocks[k]
+        return spots, blocks
+
+    def serve(j, found):
+        spots, blocks = found
         if j > 0:
             remote(cq_hbm, cqa[j], qs.at[j], qr.at[j], db=d).wait_recv()
-
-        def one(k, carry):
-            query = cqa[j][tab[0, k]]
-            keys = dbv[0, tab[1, k]]
-            vals = dbv[1, tab[1, k]]
-            lanes = lax.broadcasted_iota(jnp.int32, (SPAN, 128), 1)
-            st = jnp.zeros((SPAN, 128), jnp.float32)
+        lanes = lax.broadcasted_iota(jnp.int32, (SPAN, 128), 1)
+        st = jnp.zeros((SPAN, 128), jnp.float32)
+        out = orecv.at[0] if j == 0 else osend.at[j - 1]
+        for k in range(SLOTS):
+            query = cqa[j][spots[k]]
+            keys = dbv[0, blocks[k]]
+            vals = dbv[1, blocks[k]]
             for h in range(heads):
                 hs = slice(h * DH, (h + 1) * DH)
                 s = lax.dot_general(query[:, hs], keys[:, hs], NT, preferred_element_type=jnp.float32)
                 peak = jnp.max(s, axis=-1, keepdims=True)
                 p = jnp.exp2((s - peak) * SCALE2)
                 total = jnp.sum(p, axis=-1, keepdims=True)
-                o = jnp.dot(p.astype(jnp.bfloat16), vals[:, hs], preferred_element_type=jnp.float32) / total
-                if j == 0:
-                    orecv[0, k, :, hs] = o.astype(jnp.bfloat16)
-                else:
-                    osend[j - 1, k, :, hs] = o.astype(jnp.bfloat16)
-                st = jnp.where(lanes == h, peak * SCALE + jnp.log(total), st)
-            if j == 0:
-                stat[0, k] = st
-            else:
-                stf[k] = st
-            return carry
-
-        lax.fori_loop(0, SLOTS, one, 0)
-        if j > 0:
-            stsend[j - 1] = stf[...].reshape(SLOTS * SPAN, 128).T[:8]
+                o = jnp.dot(p.astype(jnp.bfloat16), vals[:, hs], preferred_element_type=jnp.float32) * (1.0 / total)
+                out[k, :, hs] = o.astype(jnp.bfloat16)
+                st = jnp.where(lanes == k * heads + h, peak * SCALE2 + jnp.log(total) * LOG2E, st)
+        if j == 0:
+            strecv[0] = st
+        else:
+            stsend[j - 1] = st
             out_copy(j).start()
             stat_copy(j).start()
 
@@ -296,16 +290,19 @@
         return remote(stsend.at[j - 1], strecv.at[n_d - j], ss.at[n_d - j], sr.at[n_d - j], db=(d + j) % n_d)
 
     def collect(j):
-        remote(osend.at[0], orecv.at[j], os_.at[j], or_.at[j], db=d).wait_recv()
-        remote(stsend.at[0], strecv.at[j], ss.at[j], sr.at[j], db=d).wait_recv()
-        wide = jnp.concatenate([strecv[j]] * 16, axis=0)
-        stat[j] = wide.T.reshape(SLOTS, SPAN, 128)
+        if j > 0:
+            remote(osend.at[0], orecv.at[j], os_.at[j], or_.at[j], db=d).wait_recv()
+            remote(stsend.at[0], strecv.at[j], ss.at[j], sr.at[j], db=d).wait_recv()
+        packed = strecv[j]
+        stat[j, 0] = packed
+        for k in range(1, SLOTS):
+            stat[j, k] = pltpu.roll(packed, 128 - k * heads, 1)
 
     def combine():
         places = []
         owners = []
         for n in range(entries):
-            owner = nbs[0, 0, n] // PER_SHARD
+            owner = block_id(0, n) // PER_SHARD
             rank = jnp.int32(0)
             for earlier in owners:
                 rank = rank + jnp.where(earlier == owner, 1, 0)
@@ -315,8 +312,8 @@
             (oa, ka), (ob, kb) = places[2 * u], places[2 * u + 1]
             sa, sb = stat[oa, ka], stat[ob, kb]
             peak = jnp.maximum(sa, sb)
-            ea = jnp.exp2((sa - peak) * LOG2E)
-            eb = jnp.exp2((sb - peak) * LOG2E)
+            ea = jnp.exp2(sa - peak)
+            eb = jnp.exp2(sb - peak)
             inv = 1.0 / (ea + eb)
             ea, eb = ea * inv, eb * inv
             va, vb = orecv[oa, ka], orecv[ob, kb]
@@ -386,49 +383,49 @@
 
     for n in (3, 4):
         local[n].wait()
-    serve(0)
+    serve(0, lookups(0))
     for n in (0, 1, 2):
         local[n].wait()
     attend_first()
-    move_step(0)
-
-    @pl.when(c == 1)
-    def _():
-        wait_passed(y)
-        attend(i - 1, 1)
-
-    for j in [v for v in (1, n_d - 1) if v < n_d]:
-        if j == 1 or n_d > 2:
-            serve(j)
-    for j in range(2, n_d - 1):
-        serve(j)
+    for j in range(1, n_d):
+        remote(nbv.at[0], nbv.at[j], ns.at[j], nr.at[j], db=d).wait_recv()
+        id_move(j).start()
     weight_step(0)
-    move_step(1) if half > 1 else None
+    kv_start(1)
+    found = {}
+    for j in range(1, n_d):
+        id_move(j).wait()
+        found[j] = lookups(j)
+    collect(0)
     weight_step(1)
+    serve(1, found[1])
+    weight_step(2)
+    advance(0, 0)
+    serve(3, found[3])
+    weight_step(3)
+    serve(2, found[2])
+    weight_step(4)
+    advance(0, 1)
+    pl.when(c == 1)(lambda: wait_passed(y))
+    pl.when(c == 1)(lambda: attend(i - 1, 1))
     attend_step(0)
-    weight_step(2) if half >= 2 else None
-    move_step(2) if half > 2 else None
-    if half > 1:
-        attend_step(1)
-    for step in range(3, half + 1):
-        weight_step(step)
+    advance(1, 0, 1)
+    attend_step(1)
     for j in range(1, n_d):
         collect(j)
     combine()
     weight_ready()
     local[5].wait()
     ring_start()
-    if half > 3:
-        move_step(3)
-    for step in range(1, n_x - 1):
-        ring_step(step)
-        if step == 1 and half > 2:
-            attend_step(2)
+    advance(2, 0, 1)
+    attend_step(2)
+    ring_step(1)
+    advance(3, 0, 1)
+    ring_step(2)
+    attend_step(3)
+    finish_self()
     local[6].wait()
     ring_end()
-    if half > 3:
-        attend_step(3)
-    finish_self()
     for rb in range(ROW_BLOCKS):
         rs = slice(rb * rb_rows, (rb + 1) * rb_rows)
         z_copy(rb).wait_recv()
@@ -465,6 +462,14 @@
         z_copy(rb).wait_send()
 
 
+def hand_over(a_ref, b_ref, a_out, b_out, sem):
+    copies = [pltpu.make_async_copy(a_ref, a_out, sem.at[0]), pltpu.make_async_copy(b_ref, b_out, sem.at[1])]
+    for copy in copies:
+        copy.start()
+    for copy in copies:
+        copy.wait()
+
+
 def shards(sizes, hidden_in, queries, keys, values, cross_queries, neighbours, database, out_weight):
     n_y, n_d, n_x = sizes
     half = n_y // 2
@@ -482,16 +487,15 @@
         vm((n_c, 2, rows, width), bf16),
         vm((rows, width), bf16),
         vm((rows, width), bf16),
+        pltpu.SMEM((spans, NEIGH), jnp.int32),
         vm((n_d, 8, 128), jnp.int32),
         pltpu.SMEM((n_d, 8, 128), jnp.int32),
-        pltpu.SMEM((2, SLOTS), jnp.int32),
         vm(database.shape, bf16),
         vm((n_c, n_d, piece, cols), bf16),
         vm((max(n_d - 1, 1), SLOTS, SPAN, width), bf16),
         vm((n_d, SLOTS, SPAN, width), bf16),
-        vm((SLOTS, SPAN, 128), f32),
-        vm((max(n_d - 1, 1), 8, SLOTS * SPAN), f32),
-        vm((n_d, 8, SLOTS * SPAN), f32),
+        vm((n_d - 1, SPAN, 128), f32),
+        vm((n_d, SPAN, 128), f32),
         vm((n_d, SLOTS, SPAN, 128), f32),
         vm((rows, width), bf16),
         vm((2 * (n_x - 1), rows, half_w), f32),
@@ -503,7 +507,7 @@
         vm((heads, rows, 1), f32),
         vm((heads, rows, 1), f32),
         vm((heads, rows, DH), f32),
-        dma((7,)),
+        dma((8,)),
         dma((half, 2)), dma((half, 2)), dma((half, 2)), dma((half, 2)),
         dma((n_y, 2)), dma((n_y, 2)),
         dma((n_d,)), dma((n_d,)), dma((n_d,)), dma((n_d,)), dma((n_d,)),
@@ -520,7 +524,7 @@
             jax.ShapeDtypeStruct((rows, width), bf16),
             jax.ShapeDtypeStruct((rows, half_w), bf16),
         ),
-        in_specs=[pl.BlockSpec(memory_space=pltpu.SMEM)] + [any_spec] * 7,
+        in_specs=[any_spec] * 8,
         out_specs=(pl.BlockSpec(memory_space=pltpu.VMEM), pl.BlockSpec(memory_space=pltpu.VMEM)),
         scratch_shapes=scratch,
         compiler_params=pltpu.CompilerParams(
@@ -528,7 +532,7 @@
         ),
         name="layer",
     )(
-        neighbours[0],
+        neighbours,
         hidden_in[0],
         queries[0],
         keys[0],
@@ -537,6 +541,17 @@
         database,
         out_weight.reshape(n_c, piece, cols),
     )
+    attended, mixed = pl.pallas_call(
+        hand_over,
+        out_shape=(
+            jax.ShapeDtypeStruct((rows, width), bf16),
+            jax.ShapeDtypeStruct((rows, half_w), bf16),
+        ),
+        in_specs=[pl.BlockSpec(memory_space=pltpu.VMEM)] * 2,
+        out_specs=(any_spec, any_spec),
+        scratch_shapes=[dma((2,))],
+        name="hand_over",
+    )(attended, mixed)
     return attended[None], mixed[None]
 
 

time: 130 us -> 116 us (0.89)
  the two profiles are of different devices: /device:TPU:112 before, /device:TPU:104 now
where the time goes in v2:
time: 116 us
  Pallas kernels  114 us (98%)
  local copies, waits for them, and re-layouts  1.34 us (1%)
    pallas_call x1, Pallas kernels, shards(): pl.pallas_call(functools.partial(layer, sizes), out_shape=(jax.ShapeDtype...  112 us

profile of v2, /device:TPU:104, one launch (start us, length us, event | category | flops | bytes accessed | tf_op | source)
XLA Modules:
  0.0 115.9 jit_solution(14895554675717543416)
XLA Ops:
  0.6 1.3 %copy.10.near_hbm = s32[1,4,2]{2,1,0:T(4,128)} copy(s32[1,4,2]{1,2,0:T(2,128)} %param.13) | data formatting | bytes 64 | tf_op args[5]
  2.0 111.9 %layer.1 = (bf16[256,512]{1,0:T(8,128)(2,1)}, bf16[256,512]{1,0:T(8,128)(2,1)}) custom-call(s32[1,4,2]{2,1,0:T(4,128)} %copy.10.near_hbm, bf16[256,512]{1,0:T(8,128)(2,1)} %bitcast.9, bf16[256,512]{1,0:T(8,128)(2,1)} %bitcast.10, bf16[256,512]{1,0:T(8,128)(2,1)} %bitcast.11, bf16[256,512]{1,0:T(8,128)(2,1)} %bitcast.12, bf16[4,64,512]{2,1,0:T(8,128)(2,1)} %bitcast.13, ...), custom_call_target="tpu_custom_call" | custom-call | tf_op jit(solution)/shard_map/layer/pallas_call | solution.py:521
  113.9 1.8 %hand_over.1 = (bf16[256,512]{1,0:T(8,128)(2,1)}, bf16[256,512]{1,0:T(8,128)(2,1)}) custom-call(bf16[256,512]{1,0:T(8,128)(2,1)} %get-tuple-element.6.a_ref, bf16[256,512]{1,0:T(8,128)(2,1)} %get-tuple-element.7.b_ref), custom_call_target="tpu_custom_call" | custom-call | tf_op jit(solution)/shard_map/hand_over/pallas_call | solution.py:544

commit v3 on v2

--- a/solution.py
+++ b/solution.py
@@ -14,6 +14,7 @@
 SLOTS = 4
 PER_SHARD = 8
 ROW_BLOCKS = 2
+CUTS = 1
 MESH = pl.DeviceIdType.MESH
 SCALE = 1.0 / math.sqrt(DH)
 SCALE2 = SCALE * math.log2(math.e)
@@ -121,33 +122,43 @@
         query_copy(m).start()
     kv_start(0)
 
+    def head(h):
+        return slice(h * DH, (h + 1) * DH)
+
     def attend_first():
         row = lax.broadcasted_iota(jnp.int32, (rows, rows), 0)
         col = lax.broadcasted_iota(jnp.int32, (rows, rows), 1)
         keep = col <= row
+        scores = [
+            lax.dot_general(qv[:, head(h)], kv[i, 0, :, head(h)], NT, preferred_element_type=jnp.float32)
+            for h in range(heads)
+        ]
+        weights = []
         for h in range(heads):
-            hs = slice(h * DH, (h + 1) * DH)
-            s = lax.dot_general(qv[:, hs], kv[i, 0, :, hs], NT, preferred_element_type=jnp.float32)
-            s = jnp.where(keep, s, -1e30)
+            s = jnp.where(keep, scores[h], -1e30)
             peak = jnp.max(s, axis=-1, keepdims=True)
             p = jnp.exp2((s - peak) * SCALE2)
             mref[h] = peak
             lref[h] = jnp.sum(p, axis=-1, keepdims=True)
-            acc[h] = jnp.dot(p.astype(jnp.bfloat16), kv[i, 1, :, hs], preferred_element_type=jnp.float32)
+            weights.append(p.astype(jnp.bfloat16))
+        for h in range(heads):
+            acc[h] = jnp.dot(weights[h], kv[i, 1, :, head(h)], preferred_element_type=jnp.float32)
 
     def attend(start, count):
         for h in range(heads):
-            hs = slice(h * DH, (h + 1) * DH)
-            keys = kv[pl.ds(start, count), 0, :, hs].reshape(count * rows, DH)
-            vals = kv[pl.ds(start, count), 1, :, hs].reshape(count * rows, DH)
-            s = lax.dot_general(qv[:, hs], keys, NT, preferred_element_type=jnp.float32)
-            before = mref[h]
-            peak = jnp.maximum(before, jnp.max(s, axis=-1, keepdims=True))
-            p = jnp.exp2((s - peak) * SCALE2)
-            factor = jnp.exp2((before - peak) * SCALE2)
-            mref[h] = peak
-            lref[h] = lref[h] * factor + jnp.sum(p, axis=-1, keepdims=True)
-            acc[h] = acc[h] * factor + jnp.dot(p.astype(jnp.bfloat16), vals, preferred_element_type=jnp.float32)
+            keys = kv[pl.ds(start, count), 0, :, head(h)].reshape(count * rows, DH)
+            vals = kv[pl.ds(start, count), 1, :, head(h)].reshape(count * rows, DH)
+            for part in range(CUTS):
+                rs = slice(part * rows // CUTS, (part + 1) * rows // CUTS)
+                s = lax.dot_general(qv[rs, head(h)], keys, NT, preferred_element_type=jnp.float32)
+                before = mref[h, rs]
+                peak = jnp.maximum(before, jnp.max(s, axis=-1, keepdims=True))
+                p = jnp.exp2((s - peak) * SCALE2)
+                factor = jnp.exp2((before - peak) * SCALE2)
+                mref[h, rs] = peak
+                lref[h, rs] = lref[h, rs] * factor + jnp.sum(p, axis=-1, keepdims=True)
+                fresh = jnp.dot(p.astype(jnp.bfloat16), vals, preferred_element_type=jnp.float32)
+                acc[h, rs] = acc[h, rs] * factor + fresh
 
     def wait_passed(source):
         for part in (0, 1):
@@ -263,19 +274,42 @@
         lanes = lax.broadcasted_iota(jnp.int32, (SPAN, 128), 1)
         st = jnp.zeros((SPAN, 128), jnp.float32)
         out = orecv.at[0] if j == 0 else osend.at[j - 1]
+        zero = jnp.zeros((SPAN, DH), jnp.bfloat16)
+        scores, vals = [], []
         for k in range(SLOTS):
             query = cqa[j][spots[k]]
             keys = dbv[0, blocks[k]]
-            vals = dbv[1, blocks[k]]
-            for h in range(heads):
-                hs = slice(h * DH, (h + 1) * DH)
-                s = lax.dot_general(query[:, hs], keys[:, hs], NT, preferred_element_type=jnp.float32)
-                peak = jnp.max(s, axis=-1, keepdims=True)
-                p = jnp.exp2((s - peak) * SCALE2)
-                total = jnp.sum(p, axis=-1, keepdims=True)
-                o = jnp.dot(p.astype(jnp.bfloat16), vals[:, hs], preferred_element_type=jnp.float32) * (1.0 / total)
-                out[k, :, hs] = o.astype(jnp.bfloat16)
-                st = jnp.where(lanes == k * heads + h, peak * SCALE2 + jnp.log(total) * LOG2E, st)
+            vals.append(dbv[1, blocks[k]])
+            for g in range(heads // 2):
+                first = query[:, 2 * g * DH:(2 * g + 1) * DH]
+                second = query[:, (2 * g + 1) * DH:(2 * g + 2) * DH]
+                both = jnp.concatenate(
+                    [jnp.concatenate([first, zero], axis=1), jnp.concatenate([zero, second], axis=1)], axis=0
+                )
+                scores.append(
+                    lax.dot_general(
+                        both, keys[:, 2 * g * DH:(2 * g + 2) * DH], NT, preferred_element_type=jnp.float32
+                    )
+                )
+        s = jnp.concatenate(scores, axis=0)
+        peak = jnp.max(s, axis=-1, keepdims=True)
+        p = jnp.exp2((s - peak) * SCALE2)
+        total = jnp.sum(p, axis=-1, keepdims=True)
+        inv = 1.0 / total
+        level = peak * SCALE2 + jnp.log(total) * LOG2E
+        p = p.astype(jnp.bfloat16)
+        for k in range(SLOTS):
+            for g in range(heads // 2):
+                n = k * heads + 2 * g
+                o = jnp.dot(
+                    p[n * SPAN:(n + 2) * SPAN], vals[k][:, 2 * g * DH:(2 * g + 2) * DH],
+                    preferred_element_type=jnp.float32,
+                )
+                for e in (0, 1):
+                    rs = slice((n + e) * SPAN, (n + e + 1) * SPAN)
+                    part = o[e * SPAN:(e + 1) * SPAN, e * DH:(e + 1) * DH] * inv[rs]
+                    out[k, :, (2 * g + e) * DH:(2 * g + e + 1) * DH] = part.astype(jnp.bfloat16)
+                    st = jnp.where(lanes == n + e, level[rs], st)
         if j == 0:
             strecv[0] = st
         else:

time: 116 us -> 113 us (0.974)
  Pallas kernels: 114 us -> 111 us
    pallas_call x1, Pallas kernels: 112 us -> 109 us  [shards(): pl.pallas_call(functools.partial(layer, sizes), out_shape=(jax.ShapeDtype...]
where the time goes in v3:
time: 113 us
  Pallas kernels  111 us (98%)
  local copies, waits for them, and re-layouts  1.34 us (1%)
    pallas_call x1, Pallas kernels, shards(): pl.pallas_call(functools.partial(layer, sizes), out_shape=(jax.ShapeDtype...  109 us

profile of v3, /device:TPU:104, one launch (start us, length us, event | category | flops | bytes accessed | tf_op | source)
XLA Modules:
  0.0 113.2 jit_solution(3370547737720242791)
XLA Ops:
  0.6 1.3 %copy.10.near_hbm = s32[1,4,2]{2,1,0:T(4,128)} copy(s32[1,4,2]{1,2,0:T(2,128)} %param.13) | data formatting | bytes 64 | tf_op args[5]
  2.0 109.3 %layer.1 = (bf16[256,512]{1,0:T(8,128)(2,1)}, bf16[256,512]{1,0:T(8,128)(2,1)}) custom-call(s32[1,4,2]{2,1,0:T(4,128)} %copy.10.near_hbm, bf16[256,512]{1,0:T(8,128)(2,1)} %bitcast.9, bf16[256,512]{1,0:T(8,128)(2,1)} %bitcast.10, bf16[256,512]{1,0:T(8,128)(2,1)} %bitcast.11, bf16[256,512]{1,0:T(8,128)(2,1)} %bitcast.12, bf16[4,64,512]{2,1,0:T(8,128)(2,1)} %bitcast.13, ...), custom_call_target="tpu_custom_call" | custom-call | tf_op jit(solution)/shard_map/layer/pallas_call | solution.py:555
  111.3 1.8 %hand_over.1 = (bf16[256,512]{1,0:T(8,128)(2,1)}, bf16[256,512]{1,0:T(8,128)(2,1)}) custom-call(bf16[256,512]{1,0:T(8,128)(2,1)} %get-tuple-element.6.a_ref, bf16[256,512]{1,0:T(8,128)(2,1)} %get-tuple-element.7.b_ref), custom_call_target="tpu_custom_call" | custom-call | tf_op jit(solution)/shard_map/hand_over/pallas_call | solution.py:578

commit v4 on v3

--- a/solution.py
+++ b/solution.py
@@ -34,8 +34,9 @@
     (kv, qv, hid, near_ref, nbv, nbs, dbv, wg, osend, orecv, stsend, strecv, stat, co, terms, xsend, xrecv,
      mine, zsend, zrecv, mref, lref, acc,
      loc_sem, ps, pr, ms, mr, cs, cr, qs, qr, ns, nr, nl, os_, or_, ss, sr, wzs, wzr, wps, wpr, wms, wmr, wcs, wcr,
-     xs, xr, zs, zr) = scratch[n_d:]
-    cqa = scratch[:n_d]
+     xs, xr, zs, zr) = scratch[2 * n_d - 1:]
+    hops = n_d - 1
+    own_q, cq_near = scratch[0], (scratch[1:n_d], scratch[n_d:2 * n_d - 1])
     rows = qv.shape[0]
     width = qv.shape[1]
     heads = width // DH
@@ -55,7 +56,7 @@
     across = x * 2 + 1 - zh
 
     loads = [
-        (q_hbm, qv), (k_hbm, kv.at[i, 0]), (v_hbm, kv.at[i, 1]), (cq_hbm, cqa[0]),
+        (q_hbm, qv), (k_hbm, kv.at[i, 0]), (v_hbm, kv.at[i, 1]), (cq_hbm, own_q),
         (db_hbm, dbv), (w_hbm, wg.at[:, 0]), (hid_hbm, hid), (near_hbm.at[0], near_ref),
     ]
     local = [pltpu.make_async_copy(a, b, loc_sem.at[n]) for n, (a, b) in enumerate(loads)]
@@ -78,8 +79,31 @@
     def id_copy(m):
         return remote(nbv.at[0], nbv.at[n_d - m], ns.at[n_d - m], nr.at[n_d - m], db=(d + m) % n_d)
 
-    def query_copy(m):
-        return remote(cq_hbm, cqa[n_d - m], qs.at[n_d - m], qr.at[n_d - m], db=(d + m) % n_d)
+    def there(side, hop):
+        return d - 1 - hop >= 0 if side == 0 else d + 1 + hop < n_d
+
+    def asker(side, hop):
+        return d - 1 - hop if side == 0 else d + 1 + hop
+
+    def query_copy(side, hop):
+        src = cq_hbm if hop == 0 else cq_near[side][hop - 1]
+        return remote(
+            src, cq_near[side][hop], qs.at[side, hop], qr.at[side, hop], db=d + 1 - 2 * side
+        )
+
+    def query_goes(side, hop):
+        if side == 0:
+            return jnp.logical_and(d - hop >= 0, d < n_d - 1)
+        return jnp.logical_and(d + hop < n_d, d > 0)
+
+    def query_step(hop):
+        for side in (0, 1):
+
+            @pl.when(there(side, hop))
+            def _():
+                remote(cq_hbm, cq_near[side][hop], qs.at[side, hop], qr.at[side, hop], db=d).wait_recv()
+                if hop + 1 < hops:
+                    pl.when(query_goes(side, hop + 1))(lambda: query_copy(side, hop + 1).start())
 
     def weight_copy(m):
         j = n_d - m
@@ -118,9 +142,10 @@
         id_copy(m).start()
     for m in range(1, n_d):
         weight_copy(m).start()
-    for m in range(1, n_d):
-        query_copy(m).start()
+    for side in (0, 1):
+        pl.when(query_goes(side, 0))(lambda side=side: query_copy(side, 0).start())
     kv_start(0)
+    kv_start(1)
 
     def head(h):
         return slice(h * DH, (h + 1) * DH)
@@ -250,15 +275,12 @@
     def id_move(j):
         return pltpu.make_async_copy(nbv.at[j], nbs.at[j], nl.at[j])
 
-    def block_id(j, n):
-        return near_ref[n // NEIGH, n % NEIGH] if j == 0 else nbs[j, 0, n]
-
-    def lookups(j):
+    def lookups(block_id):
         spots = [jnp.int32(0)] * SLOTS
         blocks = [jnp.int32(0)] * SLOTS
         seen = jnp.int32(0)
         for n in range(entries):
-            block = block_id(j, n)
+            block = block_id(n)
             hit = (block // PER_SHARD) == d
             for k in range(min(n + 1, SLOTS)):
                 take = jnp.logical_and(hit, seen == k)
@@ -267,17 +289,17 @@
             seen = seen + jnp.where(hit, 1, 0)
         return spots, blocks
 
-    def serve(j, found):
+    def own_id(n):
+        return near_ref[n // NEIGH, n % NEIGH]
+
+    def serve(queries, found, out, put):
         spots, blocks = found
-        if j > 0:
-            remote(cq_hbm, cqa[j], qs.at[j], qr.at[j], db=d).wait_recv()
         lanes = lax.broadcasted_iota(jnp.int32, (SPAN, 128), 1)
         st = jnp.zeros((SPAN, 128), jnp.float32)
-        out = orecv.at[0] if j == 0 else osend.at[j - 1]
         zero = jnp.zeros((SPAN, DH), jnp.bfloat16)
         scores, vals = [], []
         for k in range(SLOTS):
-            query = cqa[j][spots[k]]
+            query = queries[spots[k]]
             keys = dbv[0, blocks[k]]
             vals.append(dbv[1, blocks[k]])
             for g in range(heads // 2):
@@ -310,38 +332,50 @@
                     part = o[e * SPAN:(e + 1) * SPAN, e * DH:(e + 1) * DH] * inv[rs]
                     out[k, :, (2 * g + e) * DH:(2 * g + e + 1) * DH] = part.astype(jnp.bfloat16)
                     st = jnp.where(lanes == n + e, level[rs], st)
-        if j == 0:
-            strecv[0] = st
-        else:
-            stsend[j - 1] = st
-            out_copy(j).start()
-            stat_copy(j).start()
-
-    def out_copy(j):
-        return remote(osend.at[j - 1], orecv.at[n_d - j], os_.at[n_d - j], or_.at[n_d - j], db=(d + j) % n_d)
-
-    def stat_copy(j):
-        return remote(stsend.at[j - 1], strecv.at[n_d - j], ss.at[n_d - j], sr.at[n_d - j], db=(d + j) % n_d)
-
-    def collect(j):
-        if j > 0:
-            remote(osend.at[0], orecv.at[j], os_.at[j], or_.at[j], db=d).wait_recv()
-            remote(stsend.at[0], strecv.at[j], ss.at[j], sr.at[j], db=d).wait_recv()
-        packed = strecv[j]
-        stat[j, 0] = packed
+        put[...] = st
+
+    def serve_step(hop):
+        for side in (0, 1):
+
+            @pl.when(there(side, hop))
+            def _():
+                slot = (asker(side, hop) - d + n_d) % n_d
+                found = lookups(lambda n: nbs[slot, 0, n])
+                serve(cq_near[side][hop], found, osend.at[side, hop], stsend.at[side, hop])
+                out_copy(side, hop).start()
+                stat_copy(side, hop).start()
+
+    def out_copy(side, hop):
+        return remote(
+            osend.at[side, hop], orecv.at[d], os_.at[side, hop], or_.at[d], db=asker(side, hop)
+        )
+
+    def stat_copy(side, hop):
+        return remote(
+            stsend.at[side, hop], strecv.at[d], ss.at[side, hop], sr.at[d], db=asker(side, hop)
+        )
+
+    def collect(owner):
+        @pl.when(owner != d)
+        def _():
+            remote(osend.at[0, 0], orecv.at[owner], os_.at[0, 0], or_.at[owner], db=d).wait_recv()
+            remote(stsend.at[0, 0], strecv.at[owner], ss.at[0, 0], sr.at[owner], db=d).wait_recv()
+
+        packed = strecv[owner]
+        stat[owner, 0] = packed
         for k in range(1, SLOTS):
-            stat[j, k] = pltpu.roll(packed, 128 - k * heads, 1)
+            stat[owner, k] = pltpu.roll(packed, 128 - k * heads, 1)
 
     def combine():
         places = []
         owners = []
         for n in range(entries):
-            owner = block_id(0, n) // PER_SHARD
+            owner = own_id(n) // PER_SHARD
             rank = jnp.int32(0)
             for earlier in owners:
                 rank = rank + jnp.where(earlier == owner, 1, 0)
             owners.append(owner)
-            places.append(((owner - d + n_d) % n_d, jnp.minimum(rank, SLOTS - 1)))
+            places.append((jnp.clip(owner, 0, n_d - 1), jnp.minimum(rank, SLOTS - 1)))
         for u in range(spans):
             (oa, ka), (ob, kb) = places[2 * u], places[2 * u + 1]
             sa, sb = stat[oa, ka], stat[ob, kb]
@@ -417,49 +451,49 @@
 
     for n in (3, 4):
         local[n].wait()
-    serve(0, lookups(0))
+    serve(own_q, lookups(own_id), orecv.at[d], strecv.at[d])
+    for j in range(1, n_d):
+        remote(nbv.at[0], nbv.at[j], ns.at[j], nr.at[j], db=d).wait_recv()
+        id_move(j).start()
     for n in (0, 1, 2):
         local[n].wait()
     attend_first()
     for j in range(1, n_d):
-        remote(nbv.at[0], nbv.at[j], ns.at[j], nr.at[j], db=d).wait_recv()
-        id_move(j).start()
+        id_move(j).wait()
     weight_step(0)
-    kv_start(1)
-    found = {}
-    for j in range(1, n_d):
-        id_move(j).wait()
-        found[j] = lookups(j)
-    collect(0)
+    query_step(0)
+    serve_step(0)
     weight_step(1)
-    serve(1, found[1])
+    query_step(1)
+    serve_step(1)
     weight_step(2)
     advance(0, 0)
-    serve(3, found[3])
+    query_step(2)
+    serve_step(2)
     weight_step(3)
-    serve(2, found[2])
-    weight_step(4)
     advance(0, 1)
     pl.when(c == 1)(lambda: wait_passed(y))
     pl.when(c == 1)(lambda: attend(i - 1, 1))
     attend_step(0)
-    advance(1, 0, 1)
-    attend_step(1)
-    for j in range(1, n_d):
-        collect(j)
+    advance(1, 0)
+    weight_step(4)
+    for owner in range(n_d):
+        collect(owner)
     combine()
     weight_ready()
     local[5].wait()
     ring_start()
+    advance(1, 1)
+    attend_step(1)
+    ring_step(1)
     advance(2, 0, 1)
     attend_step(2)
-    ring_step(1)
+    ring_step(2)
+    local[6].wait()
+    ring_end()
     advance(3, 0, 1)
-    ring_step(2)
     attend_step(3)
     finish_self()
-    local[6].wait()
-    ring_end()
     for rb in range(ROW_BLOCKS):
         rs = slice(rb * rb_rows, (rb + 1) * rb_rows)
         z_copy(rb).wait_recv()
@@ -467,10 +501,12 @@
 
     for m in range(1, n_d):
         id_copy(m).wait_send()
-        query_copy(m).wait_send()
         weight_copy(m).wait_send()
-        out_copy(m).wait_send()
-        stat_copy(m).wait_send()
+    for side in (0, 1):
+        for hop in range(hops):
+            pl.when(query_goes(side, hop))(lambda side=side, hop=hop: query_copy(side, hop).wait_send())
+            pl.when(there(side, hop))(lambda side=side, hop=hop: out_copy(side, hop).wait_send())
+            pl.when(there(side, hop))(lambda side=side, hop=hop: stat_copy(side, hop).wait_send())
     for step in range(half):
         for part in (0, 1):
             if plus_has(step, part):
@@ -517,7 +553,7 @@
     bf16, f32 = jnp.bfloat16, jnp.float32
     vm, dma = pltpu.VMEM, pltpu.SemaphoreType.DMA
     any_spec = pl.BlockSpec(memory_space=pl.ANY)
-    scratch = [vm((spans, SPAN, width), bf16) for _ in range(n_d)] + [
+    scratch = [vm((spans, SPAN, width), bf16) for _ in range(2 * n_d - 1)] + [
         vm((n_c, 2, rows, width), bf16),
         vm((rows, width), bf16),
         vm((rows, width), bf16),
@@ -526,9 +562,9 @@
         pltpu.SMEM((n_d, 8, 128), jnp.int32),
         vm(database.shape, bf16),
         vm((n_c, n_d, piece, cols), bf16),
-        vm((max(n_d - 1, 1), SLOTS, SPAN, width), bf16),
+        vm((2, n_d - 1, SLOTS, SPAN, width), bf16),
         vm((n_d, SLOTS, SPAN, width), bf16),
-        vm((n_d - 1, SPAN, 128), f32),
+        vm((2, n_d - 1, SPAN, 128), f32),
         vm((n_d, SPAN, 128), f32),
         vm((n_d, SLOTS, SPAN, 128), f32),
         vm((rows, width), bf16),
@@ -544,8 +580,8 @@
         dma((8,)),
         dma((half, 2)), dma((half, 2)), dma((half, 2)), dma((half, 2)),
         dma((n_y, 2)), dma((n_y, 2)),
-        dma((n_d,)), dma((n_d,)), dma((n_d,)), dma((n_d,)), dma((n_d,)),
-        dma((n_d,)), dma((n_d,)), dma((n_d,)), dma((n_d,)),
+        dma((2, n_d - 1)), dma((2, n_d - 1)), dma((n_d,)), dma((n_d,)), dma((n_d,)),
+        dma((2, n_d - 1)), dma((n_d,)), dma((2, n_d - 1)), dma((n_d,)),
         dma((n_d,)), dma((n_d,)),
         dma((half,)), dma((half,)), dma((half,)), dma((half,)),
         dma((n_y,)), dma((n_y,)),

time: 113 us -> 100 us (0.88)
  the two profiles are of different devices: /device:TPU:104 before, /device:TPU:59 now
where the time goes in v4:
time: 100 us; the launch traced here: 99.8 us
  Pallas kernels  97.7 us (98%)
  local copies, waits for them, and re-layouts  1.34 us (1%)
    pallas_call x1, Pallas kernels, shards(): pl.pallas_call(functools.partial(layer, sizes), out_shape=(jax.ShapeDtype...  95.8 us

profile of v4, /device:TPU:59, one launch (start us, length us, event | category | flops | bytes accessed | tf_op | source)
XLA Modules:
  0.0 99.8 jit_solution(16079241745643700572)
XLA Ops:
  0.6 1.3 %copy.10.near_hbm = s32[1,4,2]{2,1,0:T(4,128)} copy(s32[1,4,2]{1,2,0:T(2,128)} %param.13) | data formatting | bytes 64 | tf_op args[5]
  2.0 95.8 %layer.1 = (bf16[256,512]{1,0:T(8,128)(2,1)}, bf16[256,512]{1,0:T(8,128)(2,1)}) custom-call(s32[1,4,2]{2,1,0:T(4,128)} %copy.10.near_hbm, bf16[256,512]{1,0:T(8,128)(2,1)} %bitcast.9, bf16[256,512]{1,0:T(8,128)(2,1)} %bitcast.10, bf16[256,512]{1,0:T(8,128)(2,1)} %bitcast.11, bf16[256,512]{1,0:T(8,128)(2,1)} %bitcast.12, bf16[4,64,512]{2,1,0:T(8,128)(2,1)} %bitcast.13, ...), custom_call_target="tpu_custom_call" | custom-call | tf_op jit(solution)/shard_map/layer/pallas_call | solution.py:591
  97.8 1.8 %hand_over.1 = (bf16[256,512]{1,0:T(8,128)(2,1)}, bf16[256,512]{1,0:T(8,128)(2,1)}) custom-call(bf16[256,512]{1,0:T(8,128)(2,1)} %get-tuple-element.6.a_ref, bf16[256,512]{1,0:T(8,128)(2,1)} %get-tuple-element.7.b_ref), custom_call_target="tpu_custom_call" | custom-call | tf_op jit(solution)/shard_map/hand_over/pallas_call | solution.py:614

commit v5 on v4

--- a/solution.py
+++ b/solution.py
@@ -31,15 +31,18 @@
 def layer(sizes, near_hbm, hid_hbm, q_hbm, k_hbm, v_hbm, cq_hbm, db_hbm, w_hbm, att_ref, mixed_ref, *scratch):
     n_y, n_d, n_x = sizes
     half = n_y // 2
-    (kv, qv, hid, near_ref, nbv, nbs, dbv, wg, osend, orecv, stsend, strecv, stat, co, terms, xsend, xrecv,
+    (kv, qv, hid, near_ref, nbv, nbs, dbv, wg, osend, orecv_a, orecv_b, stsend, strecv, stat, co, terms, xsend, xrecv,
      mine, zsend, zrecv, mref, lref, acc,
      loc_sem, ps, pr, ms, mr, cs, cr, qs, qr, ns, nr, nl, os_, or_, ss, sr, wzs, wzr, wps, wpr, wms, wmr, wcs, wcr,
      xs, xr, zs, zr) = scratch[2 * n_d - 1:]
     hops = n_d - 1
+    orecv_half = (orecv_a, orecv_b)
     own_q, cq_near = scratch[0], (scratch[1:n_d], scratch[n_d:2 * n_d - 1])
     rows = qv.shape[0]
     width = qv.shape[1]
     heads = width // DH
+    cut = SPAN // ROW_BLOCKS
+    rb_rows = rows // ROW_BLOCKS
     spans = rows // SPAN
     entries = spans * NEIGH
 
@@ -292,7 +295,7 @@
     def own_id(n):
         return near_ref[n // NEIGH, n % NEIGH]
 
-    def serve(queries, found, out, put):
+    def serve(queries, found, outs, put):
         spots, blocks = found
         lanes = lax.broadcasted_iota(jnp.int32, (SPAN, 128), 1)
         st = jnp.zeros((SPAN, 128), jnp.float32)
@@ -330,7 +333,10 @@
                 for e in (0, 1):
                     rs = slice((n + e) * SPAN, (n + e + 1) * SPAN)
                     part = o[e * SPAN:(e + 1) * SPAN, e * DH:(e + 1) * DH] * inv[rs]
-                    out[k, :, (2 * g + e) * DH:(2 * g + e + 1) * DH] = part.astype(jnp.bfloat16)
+                    for rb in range(ROW_BLOCKS):
+                        outs[rb][k, :, (2 * g + e) * DH:(2 * g + e + 1) * DH] = part[
+                            rb * cut:(rb + 1) * cut
+                        ].astype(jnp.bfloat16)
                     st = jnp.where(lanes == n + e, level[rs], st)
         put[...] = st
 
@@ -341,13 +347,20 @@
             def _():
                 slot = (asker(side, hop) - d + n_d) % n_d
                 found = lookups(lambda n: nbs[slot, 0, n])
-                serve(cq_near[side][hop], found, osend.at[side, hop], stsend.at[side, hop])
-                out_copy(side, hop).start()
+                serve(
+                    cq_near[side][hop], found, [osend.at[side, hop, rb] for rb in range(ROW_BLOCKS)],
+                    stsend.at[side, hop],
+                )
+                out_copy(side, hop, 0).start()
                 stat_copy(side, hop).start()
 
-    def out_copy(side, hop):
+    def later_half(hop):
+        for side in (0, 1):
+            pl.when(there(side, hop))(lambda side=side: out_copy(side, hop, 1).start())
+
+    def out_copy(side, hop, rb):
         return remote(
-            osend.at[side, hop], orecv.at[d], os_.at[side, hop], or_.at[d], db=asker(side, hop)
+            osend.at[side, hop, rb], orecv_half[rb].at[d], os_.at[side, hop, rb], or_.at[d, rb], db=asker(side, hop)
         )
 
     def stat_copy(side, hop):
@@ -355,18 +368,22 @@
             stsend.at[side, hop], strecv.at[d], ss.at[side, hop], sr.at[d], db=asker(side, hop)
         )
 
-    def collect(owner):
+    def collect(owner, rb):
         @pl.when(owner != d)
         def _():
-            remote(osend.at[0, 0], orecv.at[owner], os_.at[0, 0], or_.at[owner], db=d).wait_recv()
-            remote(stsend.at[0, 0], strecv.at[owner], ss.at[0, 0], sr.at[owner], db=d).wait_recv()
-
-        packed = strecv[owner]
-        stat[owner, 0] = packed
-        for k in range(1, SLOTS):
-            stat[owner, k] = pltpu.roll(packed, 128 - k * heads, 1)
-
-    def combine():
+            remote(
+                osend.at[0, 0, rb], orecv_half[rb].at[owner], os_.at[0, 0, rb], or_.at[owner, rb], db=d
+            ).wait_recv()
+            if rb == 0:
+                remote(stsend.at[0, 0], strecv.at[owner], ss.at[0, 0], sr.at[owner], db=d).wait_recv()
+
+        if rb == 0:
+            packed = strecv[owner]
+            stat[owner, 0] = packed
+            for k in range(1, SLOTS):
+                stat[owner, k] = pltpu.roll(packed, 128 - k * heads, 1)
+
+    def combine(rb):
         places = []
         owners = []
         for n in range(entries):
@@ -378,26 +395,26 @@
             places.append((jnp.clip(owner, 0, n_d - 1), jnp.minimum(rank, SLOTS - 1)))
         for u in range(spans):
             (oa, ka), (ob, kb) = places[2 * u], places[2 * u + 1]
-            sa, sb = stat[oa, ka], stat[ob, kb]
+            half_rows = pl.ds(rb * cut, cut)
+            sa, sb = stat[oa, ka, half_rows], stat[ob, kb, half_rows]
             peak = jnp.maximum(sa, sb)
             ea = jnp.exp2(sa - peak)
             eb = jnp.exp2(sb - peak)
             inv = 1.0 / (ea + eb)
             ea, eb = ea * inv, eb * inv
-            va, vb = orecv[oa, ka], orecv[ob, kb]
+            va, vb = orecv_half[rb][oa, ka], orecv_half[rb][ob, kb]
             for h in range(heads):
                 hs = slice(h * DH, (h + 1) * DH)
                 o = va[:, hs].astype(jnp.float32) * ea[:, h:h + 1] + vb[:, hs].astype(jnp.float32) * eb[:, h:h + 1]
-                co[u * SPAN:(u + 1) * SPAN, hs] = o.astype(jnp.bfloat16)
+                co[rb * rb_rows + u * cut:rb * rb_rows + (u + 1) * cut, hs] = o.astype(jnp.bfloat16)
 
     half_w = terms.shape[2]
 
-    def project(rho, side):
+    def project(rho, side, rb):
         j = ((x + rho) % n_x - d + n_d) % n_d
         block = wg[:, j, :, side * half_w:(side + 1) * half_w].reshape(width, half_w)
-        return jnp.dot(co[...], block, preferred_element_type=jnp.float32)
-
-    rb_rows = rows // ROW_BLOCKS
+        return jnp.dot(co[rb * rb_rows:(rb + 1) * rb_rows], block, preferred_element_type=jnp.float32)
+
 
     def ring_copy(side, step, rb):
         rs = pl.ds(rb * rb_rows, rb_rows)
@@ -409,40 +426,40 @@
     def rho_of(side, step):
         return (n_x - 1 - step) % n_x if side == 0 else (1 + step) % n_x
 
-    def ring_start():
+    def ring_start(rb):
+        rs = slice(rb * rb_rows, (rb + 1) * rb_rows)
         for side in (0, 1):
-            xsend[side, 0] = project(rho_of(side, 0), side).astype(jnp.bfloat16)
-            for rb in range(ROW_BLOCKS):
-                ring_copy(side, 0, rb).start()
+            xsend[side, 0, rs] = project(rho_of(side, 0), side, rb).astype(jnp.bfloat16)
+            ring_copy(side, 0, rb).start()
         for step in range(1, n_x):
             for side in (0, 1):
-                terms[side * (n_x - 1) + step - 1] = project(rho_of(side, step), side)
-
-    def ring_step(step):
-        for rb in range(ROW_BLOCKS):
-            rs = slice(rb * rb_rows, (rb + 1) * rb_rows)
-            for side in (0, 1):
-                ring_copy(side, step - 1, rb).wait_recv()
-                total = xrecv[side, step - 1, rs].astype(jnp.float32) + terms[side * (n_x - 1) + step - 1, rs]
-                xsend[side, step, rs] = total.astype(jnp.bfloat16)
-                ring_copy(side, step, rb).start()
+                terms[side * (n_x - 1) + step - 1, rs] = project(rho_of(side, step), side, rb)
+
+    def ring_step(step, rb):
+        rs = slice(rb * rb_rows, (rb + 1) * rb_rows)
+        for side in (0, 1):
+            ring_copy(side, step - 1, rb).wait_recv()
+            total = xrecv[side, step - 1, rs].astype(jnp.float32) + terms[side * (n_x - 1) + step - 1, rs]
+            xsend[side, step, rs] = total.astype(jnp.bfloat16)
+            ring_copy(side, step, rb).start()
 
     def z_copy(rb):
         rs = pl.ds(rb * rb_rows, rb_rows)
         return remote(zsend.at[rs], zrecv.at[rs], zs.at[rb], zr.at[rb], tp=across)
 
-    def ring_end():
-        for rb in range(ROW_BLOCKS):
-            rs = slice(rb * rb_rows, (rb + 1) * rb_rows)
-            sums = []
-            for side in (0, 1):
-                ring_copy(side, n_x - 2, rb).wait_recv()
-                sums.append(
-                    xrecv[side, n_x - 2, rs].astype(jnp.float32) + terms[side * (n_x - 1) + n_x - 2, rs]
-                )
-            zsend[rs] = jnp.where(zh == 0, sums[1], sums[0]).astype(jnp.bfloat16)
-            z_copy(rb).start()
-            mine[rs] = jnp.where(zh == 0, sums[0], sums[1]) + hid[rs].astype(jnp.float32)
+    def span_rows(u, rb):
+        return slice(u * SPAN + rb * cut, u * SPAN + (rb + 1) * cut)
+
+    def ring_end(rb):
+        rs = slice(rb * rb_rows, (rb + 1) * rb_rows)
+        sums = []
+        for side in (0, 1):
+            ring_copy(side, n_x - 2, rb).wait_recv()
+            sums.append(xrecv[side, n_x - 2, rs].astype(jnp.float32) + terms[side * (n_x - 1) + n_x - 2, rs])
+        zsend[rs] = jnp.where(zh == 0, sums[1], sums[0]).astype(jnp.bfloat16)
+        z_copy(rb).start()
+        before = jnp.concatenate([hid[span_rows(u, rb)] for u in range(spans)], axis=0)
+        mine[rs] = jnp.where(zh == 0, sums[0], sums[1]) + before.astype(jnp.float32)
 
     def finish_self():
         for h in range(heads):
@@ -451,7 +468,7 @@
 
     for n in (3, 4):
         local[n].wait()
-    serve(own_q, lookups(own_id), orecv.at[d], strecv.at[d])
+    serve(own_q, lookups(own_id), [ref.at[d] for ref in orecv_half], strecv.at[d])
     for j in range(1, n_d):
         remote(nbv.at[0], nbv.at[j], ns.at[j], nr.at[j], db=d).wait_recv()
         id_move(j).start()
@@ -466,10 +483,13 @@
     weight_step(1)
     query_step(1)
     serve_step(1)
+    later_half(0)
     weight_step(2)
     advance(0, 0)
     query_step(2)
     serve_step(2)
+    later_half(1)
+    later_half(2)
     weight_step(3)
     advance(0, 1)
     pl.when(c == 1)(lambda: wait_passed(y))
@@ -478,26 +498,35 @@
     advance(1, 0)
     weight_step(4)
     for owner in range(n_d):
-        collect(owner)
-    combine()
+        collect(owner, 0)
+    combine(0)
     weight_ready()
     local[5].wait()
-    ring_start()
+    ring_start(0)
     advance(1, 1)
+    for owner in range(n_d):
+        collect(owner, 1)
+    combine(1)
+    ring_step(1, 0)
+    ring_start(1)
     attend_step(1)
-    ring_step(1)
+    ring_step(2, 0)
+    ring_step(1, 1)
+    local[6].wait()
+    ring_end(0)
     advance(2, 0, 1)
+    ring_step(2, 1)
     attend_step(2)
-    ring_step(2)
-    local[6].wait()
-    ring_end()
+    ring_end(1)
     advance(3, 0, 1)
     attend_step(3)
     finish_self()
     for rb in range(ROW_BLOCKS):
         rs = slice(rb * rb_rows, (rb + 1) * rb_rows)
         z_copy(rb).wait_recv()
-        mixed_ref[rs] = (mine[rs] + zrecv[rs].astype(jnp.float32)).astype(jnp.bfloat16)
+        whole = (mine[rs] + zrecv[rs].astype(jnp.float32)).astype(jnp.bfloat16)
+        for u in range(spans):
+            mixed_ref[span_rows(u, rb)] = whole[u * cut:(u + 1) * cut]
 
     for m in range(1, n_d):
         id_copy(m).wait_send()
@@ -505,7 +534,7 @@
     for side in (0, 1):
         for hop in range(hops):
             pl.when(query_goes(side, hop))(lambda side=side, hop=hop: query_copy(side, hop).wait_send())
-            pl.when(there(side, hop))(lambda side=side, hop=hop: out_copy(side, hop).wait_send())
+            pl.when(there(side, hop))(lambda side=side, hop=hop: [out_copy(side, hop, rb).wait_send() for rb in range(ROW_BLOCKS)] and None)
             pl.when(there(side, hop))(lambda side=side, hop=hop: stat_copy(side, hop).wait_send())
     for step in range(half):
         for part in (0, 1):
@@ -562,8 +591,9 @@
         pltpu.SMEM((n_d, 8, 128), jnp.int32),
         vm(database.shape, bf16),
         vm((n_c, n_d, piece, cols), bf16),
-        vm((2, n_d - 1, SLOTS, SPAN, width), bf16),
-        vm((n_d, SLOTS, SPAN, width), bf16),
+        vm((2, n_d - 1, ROW_BLOCKS, SLOTS, SPAN // ROW_BLOCKS, width), bf16),
+        vm((n_d, SLOTS, SPAN // ROW_BLOCKS, width), bf16),
+        vm((n_d, SLOTS, SPAN // ROW_BLOCKS, width), bf16),
         vm((2, n_d - 1, SPAN, 128), f32),
         vm((n_d, SPAN, 128), f32),
         vm((n_d, SLOTS, SPAN, 128), f32),
@@ -581,7 +611,7 @@
         dma((half, 2)), dma((half, 2)), dma((half, 2)), dma((half, 2)),
         dma((n_y, 2)), dma((n_y, 2)),
         dma((2, n_d - 1)), dma((2, n_d - 1)), dma((n_d,)), dma((n_d,)), dma((n_d,)),
-        dma((2, n_d - 1)), dma((n_d,)), dma((2, n_d - 1)), dma((n_d,)),
+        dma((2, n_d - 1, ROW_BLOCKS)), dma((n_d, ROW_BLOCKS)), dma((2, n_d - 1)), dma((n_d,)),
         dma((n_d,)), dma((n_d,)),
         dma((half,)), dma((half,)), dma((half,)), dma((half,)),
         dma((n_y,)), dma((n_y,)),

time: 100 us -> 94.4 us (0.944)
  the two profiles are of different devices: /device:TPU:59 before, /device:TPU:49 now
where the time goes in v5:
time: 94.4 us; the launch traced here: 94.3 us
  Pallas kernels  92.2 us (98%)
  local copies, waits for them, and re-layouts  1.34 us (1%)
    pallas_call x1, Pallas kernels, shards(): pl.pallas_call(functools.partial(layer, sizes), out_shape=(jax.ShapeDtype...  90.3 us

profile of v5, /device:TPU:49, one launch (start us, length us, event | category | flops | bytes accessed | tf_op | source)
XLA Modules:
  0.0 94.3 jit_solution(3907161041049460604)
XLA Ops:
  0.6 1.3 %copy.10.near_hbm = s32[1,4,2]{2,1,0:T(4,128)} copy(s32[1,4,2]{1,2,0:T(2,128)} %param.13) | data formatting | bytes 64 | tf_op args[5]
  2.0 90.3 %layer.1 = (bf16[256,512]{1,0:T(8,128)(2,1)}, bf16[256,512]{1,0:T(8,128)(2,1)}) custom-call(s32[1,4,2]{2,1,0:T(4,128)} %copy.10.near_hbm, bf16[256,512]{1,0:T(8,128)(2,1)} %bitcast.9, bf16[256,512]{1,0:T(8,128)(2,1)} %bitcast.10, bf16[256,512]{1,0:T(8,128)(2,1)} %bitcast.11, bf16[256,512]{1,0:T(8,128)(2,1)} %bitcast.12, bf16[4,64,512]{2,1,0:T(8,128)(2,1)} %bitcast.13, ...), custom_call_target="tpu_custom_call" | custom-call | tf_op jit(solution)/shard_map/layer/pallas_call | solution.py:621
  92.3 1.8 %hand_over.1 = (bf16[256,512]{1,0:T(8,128)(2,1)}, bf16[256,512]{1,0:T(8,128)(2,1)}) custom-call(bf16[256,512]{1,0:T(8,128)(2,1)} %get-tuple-element.6.a_ref, bf16[256,512]{1,0:T(8,128)(2,1)} %get-tuple-element.7.b_ref), custom_call_target="tpu_custom_call" | custom-call | tf_op jit(solution)/shard_map/hand_over/pallas_call | solution.py:644

commit v6 on v5

--- a/solution.py
+++ b/solution.py
@@ -148,7 +148,6 @@
     for side in (0, 1):
         pl.when(query_goes(side, 0))(lambda side=side: query_copy(side, 0).start())
     kv_start(0)
-    kv_start(1)
 
     def head(h):
         return slice(h * DH, (h + 1) * DH)
@@ -478,6 +477,7 @@
     for j in range(1, n_d):
         id_move(j).wait()
     weight_step(0)
+    kv_start(1)
     query_step(0)
     serve_step(0)
     weight_step(1)
@@ -485,13 +485,12 @@
     serve_step(1)
     later_half(0)
     weight_step(2)
-    advance(0, 0)
     query_step(2)
     serve_step(2)
     later_half(1)
     later_half(2)
     weight_step(3)
-    advance(0, 1)
+    advance(0, 0, 1)
     pl.when(c == 1)(lambda: wait_passed(y))
     pl.when(c == 1)(lambda: attend(i - 1, 1))
     attend_step(0)

time: 94.4 us -> 97.5 us (1.033)
  the two profiles are of different devices: /device:TPU:49 before, /device:TPU:59 now
where the time goes in v6:
time: 97.5 us; the launch traced here: 97.4 us
  Pallas kernels  95.2 us (98%)
  local copies, waits for them, and re-layouts  1.34 us (1%)
    pallas_call x1, Pallas kernels, shards(): pl.pallas_call(functools.partial(layer, sizes), out_shape=(jax.ShapeDtype...  93.4 us

profile of v6, /device:TPU:59, one launch (start us, length us, event | category | flops | bytes accessed | tf_op | source)
XLA Modules:
  0.0 97.4 jit_solution(18021427483298703393)
XLA Ops:
  0.6 1.3 %copy.10.near_hbm = s32[1,4,2]{2,1,0:T(4,128)} copy(s32[1,4,2]{1,2,0:T(2,128)} %param.13) | data formatting | bytes 64 | tf_op args[5]
  2.0 93.4 %layer.1 = (bf16[256,512]{1,0:T(8,128)(2,1)}, bf16[256,512]{1,0:T(8,128)(2,1)}) custom-call(s32[1,4,2]{2,1,0:T(4,128)} %copy.10.near_hbm, bf16[256,512]{1,0:T(8,128)(2,1)} %bitcast.9, bf16[256,512]{1,0:T(8,128)(2,1)} %bitcast.10, bf16[256,512]{1,0:T(8,128)(2,1)} %bitcast.11, bf16[256,512]{1,0:T(8,128)(2,1)} %bitcast.12, bf16[4,64,512]{2,1,0:T(8,128)(2,1)} %bitcast.13, ...), custom_call_target="tpu_custom_call" | custom-call | tf_op jit(solution)/shard_map/layer/pallas_call | solution.py:620
  95.4 1.8 %hand_over.1 = (bf16[256,512]{1,0:T(8,128)(2,1)}, bf16[256,512]{1,0:T(8,128)(2,1)}) custom-call(bf16[256,512]{1,0:T(8,128)(2,1)} %get-tuple-element.6.a_ref, bf16[256,512]{1,0:T(8,128)(2,1)} %get-tuple-element.7.b_ref), custom_call_target="tpu_custom_call" | custom-call | tf_op jit(solution)/shard_map/hand_over/pallas_call | solution.py:643
